TPU v7x, 32 devices: a whole 2x2x4 slice. The times are simulated.
32 devices in a mesh: groups: 2 (over y), space: 4 (over z), tm: 2 (over x), chan: 2 (over core).
Axes of the slice: x: 2, y: 2, z: 4, core: 2. Of those that a mesh axis runs over, the one named last changes fastest.
Arguments:
- features: float32 [48, 40, 384], P(('groups', 'space'), 'tm'), parts along dimension 0, may hold values from -50 to 50
- norm1_gain: float32 [384], replicated, may hold values from 0.25 to 1.75
- norm1_shift: float32 [384], replicated, may hold values from -3 to 3
- conv1_weight: float32 [3, 3, 384, 384], P(None, None, 'space', 'chan'), may hold values from -0.109375 to 0.109375
- norm2_gain: float32 [384], replicated, may hold values from 0.25 to 1.75
- norm2_shift: float32 [384], replicated, may hold values from -3 to 3
- conv2_weight: float32 [3, 3, 384, 384], P(None, None, 'space', 'chan'), may hold values from -0.109375 to 0.109375
- head_gain: float32 [384], replicated, may hold values from 0.25 to 1.75
- head_shift: float32 [384], replicated, may hold values from -3 to 3
- head_weight: float32 [3, 3, 384, 16], P(None, None, 'space', 'chan'), may hold values from -0.109375 to 0.109375
- head_bias: float32 [16], P('chan'), may hold values from -3 to 3
- noisy_latents: float32 [4, 16, 24, 40], P(('groups', 'tm'), None, 'space'), parts along dimension 0, may hold values from -6 to 6
- later_cond: float32 [4, 16, 24, 40], P(('groups', 'tm'), None, 'space'), parts along dimension 0, may hold values from -6 to 6
- patch_weight: float32 [144, 5120], P(None, 'chan'), may hold values from -0.5 to 0.5
- patch_bias: float32 [5120], P('chan'), may hold values from -3 to 3
Outputs:
- tokens: float32 [4, 12, 20, 5120], P(('groups', 'tm'), 'space', None, 'chan'), parts along dimension 0
- image_latent: float32 [48, 40, 16], P(('groups', 'space'), 'tm'), parts along dimension 0
There are 2 independent parts, one for each index of `groups`. A program takes and returns all parts, laid end to end along the dimension named above; an argument that names none is the same for every part. Nothing has to cross between parts.
All inputs are finite; a program needn't handle non-finite values.
Results may differ from a plain program's by a relative error of at most 0.00007.
Values sent between devices are 32-bit elements; how exact they have to be, the bound alone decides.
A program may use at most 64 MiB of HBM per device.

v0:
```python
import functools

import jax
import jax.numpy as jnp
from jax import lax
from jax.experimental import pallas as pl
from jax.experimental.pallas import tpu as pltpu
from jax.sharding import PartitionSpec as P

NGROUP = 32


EPSILON = 1e-06
HIGHEST = lax.Precision.HIGHEST


def padded_2(cells, sides, width):
    for axis, dim in sides:
        count = lax.axis_size(axis)
        ends = count - 1
        head = lax.slice_in_dim(cells, 0, width, axis=dim)
        tail = lax.slice_in_dim(cells, cells.shape[dim] - width, cells.shape[dim], axis=dim)
        cells = jnp.concatenate(
            [
                lax.ppermute(tail, axis, [(i, (i + 1) % count) for i in range(ends)]),
                cells,
                lax.ppermute(head, axis, [((i + 1) % count, i) for i in range(ends)]),
            ],
            axis=dim,
        )
    return cells


def group_stats(inner, count_all):
    grouped = inner.reshape(-1, NGROUP, inner.shape[-1] // NGROUP)
    totals, squares = lax.psum(
        (jnp.sum(grouped, axis=(0, 2)), jnp.sum(grouped * grouped, axis=(0, 2))), ("space", "tm")
    )
    center = totals / count_all
    spread = squares / count_all - center * center
    return (center, lax.rsqrt(spread + EPSILON))


def normalize_act(values, stats, gain, shift):
    center, inverse = stats
    grouped = values.reshape(values.shape[:-1] + (NGROUP, values.shape[-1] // NGROUP))
    scaled = (grouped - center[:, None]) * inverse[:, None]
    return jax.nn.silu(scaled.reshape(values.shape) * gain + shift)


def tap_columns(padded, rows_out, cols_out):
    shifted = [
        padded[row_tap : row_tap + rows_out, col_tap : col_tap + cols_out, :]
        for row_tap in range(3)
        for col_tap in range(3)
    ]
    return jnp.stack(shifted, axis=2).reshape(rows_out * cols_out, 9, padded.shape[-1])


def add_taps(columns, piece):
    depth = piece.shape[2]
    picked = columns.reshape(columns.shape[0], 9 * depth)
    return jnp.dot(
        picked,
        piece.reshape(9 * depth, piece.shape[3]),
        precision=HIGHEST,
        preferred_element_type=jnp.float32,
    )


def wide_conv(padded, weight, rows_out, cols_out):
    columns = tap_columns(padded, rows_out, cols_out)
    summed = add_taps(columns, lax.all_gather(weight, "space", axis=2, tiled=True))
    return lax.all_gather(summed.reshape(rows_out, cols_out, -1), "chan", axis=2, tiled=True)


def border_rim(values):
    return padded_2(values, (("space", 0), ("tm", 1)), 1)


def on_device(
    features,
    norm1_gain,
    norm1_shift,
    conv1_weight,
    norm2_gain,
    norm2_shift,
    conv2_weight,
    head_gain,
    head_shift,
    head_weight,
    head_bias,
    noisy_latents,
    later_cond,
    patch_weight,
    patch_bias,
):
    tile_rows = features.shape[0]
    tile_cols = features.shape[1]
    count_all = float(
        tile_rows
        * tile_cols
        * lax.axis_size("space")
        * lax.axis_size("tm")
        * (features.shape[2] // NGROUP)
    )
    first_stats = group_stats(features, count_all)
    active = normalize_act(features, first_stats, norm1_gain, norm1_shift)
    first_conv = wide_conv(border_rim(active), conv1_weight, tile_rows, tile_cols)
    second_stats = group_stats(first_conv, count_all)
    second_act = normalize_act(first_conv, second_stats, norm2_gain, norm2_shift)
    second_conv = wide_conv(border_rim(second_act), conv2_weight, tile_rows, tile_cols)
    hidden = features + second_conv
    head_stats = group_stats(hidden, count_all)
    head_act = normalize_act(hidden, head_stats, head_gain, head_shift)
    head_pad = padded_2(head_act, (("space", 0), ("tm", 1)), 1)
    head_columns = tap_columns(head_pad, tile_rows, tile_cols)
    latent_part = (
        add_taps(head_columns, lax.all_gather(head_weight, "space", axis=2, tiled=True)) + head_bias
    )
    image_latent = lax.all_gather(
        latent_part.reshape(tile_rows, tile_cols, -1), "chan", axis=2, tiled=True
    )
    latent_row = lax.all_gather(image_latent, "tm", axis=1, tiled=True)
    frame_count = noisy_latents.shape[0]
    full_width = noisy_latents.shape[3]
    frame_ids = lax.axis_index("tm") * frame_count + jnp.arange(frame_count)
    opening = frame_ids == 0
    condition = jnp.where(
        opening[:, None, None, None], jnp.transpose(latent_row, (2, 0, 1))[None], later_cond
    )
    marks = jnp.broadcast_to(
        opening.astype(jnp.float32)[:, None, None, None], (frame_count, 4, tile_rows, full_width)
    )
    stacked = jnp.concatenate([noisy_latents, marks, condition], axis=1)
    channel_count = stacked.shape[1]
    patches = (
        stacked.reshape(frame_count, channel_count, tile_rows // 2, 2, full_width // 2, 2)
        .transpose(0, 2, 4, 1, 3, 5)
        .reshape(-1, channel_count * 4)
    )
    tokens = (
        jnp.dot(patches, patch_weight, precision=HIGHEST, preferred_element_type=jnp.float32)
        + patch_bias
    )
    return (tokens.reshape(frame_count, tile_rows // 2, full_width // 2, -1), image_latent)


MESH = pl.DeviceIdType.MESH
LANES = 128
BF16 = jnp.bfloat16
F32 = jnp.float32


def split_pair(values):
    high = values.astype(BF16)
    return high, (values - high.astype(F32)).astype(BF16)


def split_columns(values):
    high, low = split_pair(values)
    return jnp.concatenate([high, low, high], axis=1)


def finish_kernel(dims, patch, base, wc, latent_in, tokens, latent):
    PC, PP, Z = dims["PC"], dims["PP"], dims["Z"]
    for f in range(dims["FR"]):
        lhs = split_columns(patch[f, :, 0 : 4 * Z])
        got = base[f] + jnp.dot(lhs, wc[...], preferred_element_type=F32)
        for p in range(dims["PR"]):
            tokens[p, :, f, :] = got[p * PP : p * PP + PC, :]
    latent[...] = latent_in[...]


def fused_kernel(
    dims,
    feat_hbm,
    gain1_hbm,
    shift1_hbm,
    w1_hbm,
    gain2_hbm,
    shift2_hbm,
    w2_hbm,
    gain3_hbm,
    shift3_hbm,
    head_w_hbm,
    head_b_hbm,
    noisy_hbm,
    later_hbm,
    pw_hbm,
    patch_b_hbm,
    patch_out,
    base_out,
    wc_out,
    latent,
    feat,
    gain1,
    shift1,
    gain2,
    shift2,
    gain3,
    shift3,
    head_w,
    head_b,
    noisy,
    later,
    patch_b,
    w1_raw,
    w2_raw,
    pw_raw,
    w1_mat,
    w2_mat,
    wh_mat,
    mixed,
    wn_mat,
    wc_mat,
    base,
    a_send,
    a_pack,
    a_in,
    rim,
    rim_in,
    feat_all,
    conv_all,
    taps,
    msg,
    msg_in,
    piece,
    piece_in,
    lat_send,
    lat_in,
    cells,
    turned,
    patch,
    load_sem,
    a_ssem,
    a_rsem,
    f_ssem,
    f_rsem,
    r_ssem,
    r_rsem,
    m_ssem,
    m_rsem,
    sib_ssem,
    sib_rsem,
    p_ssem,
    p_rsem,
    l_ssem,
    l_rsem,
):
    S, T, C = dims["S"], dims["T"], dims["C"]
    R, W, CH = dims["R"], dims["W"], dims["CH"]
    Z, FR = dims["Z"], dims["FR"]
    CB = CH // S
    NH = CH // C
    BH = NH // CB
    H = S * R
    M = H * W
    HM = M // 2
    HR = H // 2
    TILE = R * W
    per_group = CH // NGROUP
    ZH = Z // C
    s = lax.axis_index("space")
    t = lax.axis_index("tm")
    c = lax.axis_index("chan")
    other = 1 - c

    early = (
        (feat_hbm, feat), (w1_hbm, w1_raw), (gain1_hbm, gain1), (shift1_hbm, shift1),
        (w2_hbm, w2_raw), (gain2_hbm, gain2), (shift2_hbm, shift2),
        (gain3_hbm, gain3), (shift3_hbm, shift3), (head_w_hbm, head_w), (head_b_hbm, head_b),
        (noisy_hbm, noisy), (later_hbm, later), (patch_b_hbm, patch_b),
    )
    loads = [
        pltpu.make_async_copy(src, dst, load_sem.at[k]) for k, (src, dst) in enumerate(early)
    ]
    strips = pw_raw.shape[0]
    loads += [
        pltpu.make_async_copy(
            pw_hbm.at[:, n * LANES : (n + 1) * LANES], pw_raw.at[n], load_sem.at[len(early) + n]
        )
        for n in range(strips)
    ]
    for load in loads:
        load.start()

    barrier = pltpu.get_barrier_semaphore()
    for ds in range(S):
        for dt in range(T):
            for dc in range(C):
                if ds or dt or dc:
                    pl.semaphore_signal(
                        barrier,
                        inc=1,
                        device_id={
                            "space": lax.rem(s + ds, S),
                            "tm": lax.rem(t + dt, T),
                            "chan": lax.rem(c + dc, C),
                        },
                        device_id_type=MESH,
                    )

    def padded(values, width):
        rows = values.shape[0]
        if width == values.shape[1]:
            return values
        return jnp.concatenate([values, jnp.zeros((rows, width - values.shape[1]), values.dtype)], axis=1)

    loads[0].wait()
    for r in range(R):
        line = feat[r]
        for j in range(S):
            a_send[j, r * W : (r + 1) * W, :] = padded(line[:, j * CB : (j + 1) * CB], LANES)

    def pack(dst, value, main):
        rows = value.shape[0]
        dst[...] = value[0:main]
        rest = rows - main
        free = LANES - CB
        for j in range(CB // free if rest else 0):
            dst[j * rest : (j + 1) * rest, CB:LANES] = value[main:rows, j * free : (j + 1) * free]

    def unpack(value, rows):
        main = value.shape[0]
        rest = rows - main
        if not rest:
            return (value,)
        free = LANES - CB
        columns = [value[j * rest : (j + 1) * rest, CB:LANES] for j in range(CB // free)]
        return value, padded(jnp.concatenate(columns, axis=1), LANES)

    def channel_stats(values):
        total = jnp.sum(values, axis=0, keepdims=True)
        middle = total * (1.0 / values.shape[0])
        away = values - middle
        return total, jnp.sum(away * away, axis=0, keepdims=True)

    AM, PM, RE = dims["AM"], dims["PM"], dims["RE"]
    AH = AM // 2
    for j in range(S):
        pack(a_pack.at[j], a_send[j], AM)

    pl.semaphore_wait(barrier, S * T * C - 1)

    def a_copy(step, sent):
        peer = lax.rem(s + step, S)
        slot = s if sent else peer
        mine = pl.ds(pl.multiple_of(c * AH, 8), AH)
        return pltpu.make_async_remote_copy(
            src_ref=a_pack.at[peer, mine],
            dst_ref=a_in.at[slot, mine],
            send_sem=a_ssem.at[peer],
            recv_sem=a_rsem.at[slot],
            device_id={"space": peer},
            device_id_type=MESH,
        )

    def a_forward(step, half):
        source = lax.rem(s + step, S)
        rows = pl.ds(pl.multiple_of(half * AH, 8), AH)
        return pltpu.make_async_remote_copy(
            src_ref=a_in.at[source, rows],
            dst_ref=a_in.at[source, rows],
            send_sem=f_ssem.at[source],
            recv_sem=f_rsem.at[source],
            device_id={"chan": other},
            device_id_type=MESH,
        )

    def rim_copy(dt, j, sent):
        peer = lax.rem(t + dt, T)
        slot_t, slot_s = (t, s) if sent else (peer, j)
        return pltpu.make_async_remote_copy(
            src_ref=rim.at[j],
            dst_ref=rim_in.at[slot_t, slot_s],
            send_sem=r_ssem.at[peer, j],
            recv_sem=r_rsem.at[slot_t, slot_s],
            device_id={"space": j, "tm": peer},
            device_id_type=MESH,
        )

    for step in range(1, S):
        a_copy(step, True).start()
    for j in range(S):
        total, spread = channel_stats(a_send[j])
        rim[j, 0:R, :] = a_send[j, pl.ds(0, R, stride=W), :]
        rim[j, RE : RE + R, :] = a_send[j, pl.ds(W - 1, R, stride=W), :]
        rim[j, 2 * RE : 2 * RE + 1, :] = total
        rim[j, 2 * RE + 1 : 2 * RE + 2, :] = spread
    for dt in range(1, T):
        for j in range(S):
            rim_copy(dt, j, True).start()
    feat_all[pl.ds(pl.multiple_of(s * TILE, 8), TILE), :] = a_send[s]

    def pick_block(ref):
        row = ref[...].reshape(1, CH)
        out = jnp.zeros((1, CB), F32)
        for j in range(S):
            out = jnp.where(s == j, row[:, j * CB : (j + 1) * CB], out)
        return padded(out, LANES)

    row_id = lax.broadcasted_iota(jnp.int32, (LANES, LANES), 0)
    col_id = lax.broadcasted_iota(jnp.int32, (LANES, LANES), 1)
    same = ((row_id // per_group) == (col_id // per_group)) & (row_id < CB) & (col_id < CB)
    member = jnp.where(same, 1.0, 0.0).astype(F32)

    def group_sum(row):
        wide = jnp.broadcast_to(row, (8, LANES))
        return jnp.dot(wide, member, precision=HIGHEST, preferred_element_type=F32)[0:1]

    def prepare(raw, mat):
        gap = jnp.zeros((LANES - CB, BH * LANES), BF16) if CB < LANES else None
        for tap in range(9):
            w = raw[tap]
            wide = jnp.concatenate(
                [padded(w[:, i * CB : (i + 1) * CB], LANES) for i in range(BH)], axis=1
            )
            high, low = split_pair(wide)
            store_split(mat, tap, high, low, gap)

    def store_split(mat, tap, high, low, gap):
        for place, value in ((2 * tap, high), (2 * tap + 1, high), (18 + tap, low)):
            mat[place * LANES : place * LANES + CB, :] = value
            if gap is not None:
                mat[place * LANES + CB : (place + 1) * LANES, :] = gap

    edge = HR
    pad_edge = dims["EDGE"]

    def exchange(k, full):
        start = pl.multiple_of(c * HM, 8)
        total, spread = channel_stats(full[pl.ds(start, HM), :])
        msg[k, 0:edge, :] = full[pl.ds(start, HR, stride=W), :]
        msg[k, pad_edge : pad_edge + edge, :] = full[pl.ds(start + (W - 1), HR, stride=W), :]
        msg[k, 2 * pad_edge : 2 * pad_edge + 1, :] = total
        msg[k, 2 * pad_edge + 1 : 2 * pad_edge + 2, :] = spread

        def copies(slot_t, slot_c, peer_t, peer_c, dc):
            return pltpu.make_async_remote_copy(
                src_ref=msg.at[k],
                dst_ref=msg_in.at[k, slot_t, slot_c],
                send_sem=m_ssem.at[k, peer_t, peer_c],
                recv_sem=m_rsem.at[k, slot_t, slot_c],
                device_id={"tm": peer_t, "chan": peer_c},
                device_id_type=MESH,
            )

        outgoing = []
        incoming = []
        for dt in range(1, T):
            for dc in range(C):
                peer_t = lax.rem(t + dt, T)
                peer_c = lax.rem(c + dc, C)
                outgoing.append(copies(t, c, peer_t, peer_c, dc))
                incoming.append(copies(peer_t, peer_c, peer_t, peer_c, dc))
        for copy in outgoing:
            copy.start()
        return outgoing, incoming

    def sibling(k, full, mine):
        start = pl.multiple_of(mine * HM, 8)
        return pltpu.make_async_remote_copy(
            src_ref=full.at[pl.ds(start, HM)],
            dst_ref=full.at[pl.ds(start, HM)],
            send_sem=sib_ssem.at[k],
            recv_sem=sib_rsem.at[k],
            device_id={"chan": other},
            device_id_type=MESH,
        )

    left = lax.rem(t + T - 1, T)
    right = lax.rem(t + 1, T)

    def activate(full, remote, rims, gain, shift):
        parts = [channel_stats(full[h * HM : (h + 1) * HM, :]) + (HM,) for h in range(2)]
        parts += remote
        scale = 1.0 / float(per_group * M * T)
        total = parts[0][0]
        for part in parts[1:]:
            total = total + part[0]
        center = group_sum(total) * scale
        gathered = jnp.zeros((1, LANES), F32)
        for part_total, part_spread, count in parts:
            away = part_total * (1.0 / count) - center
            gathered = gathered + part_spread + away * away * float(count)
        inverse = lax.rsqrt(group_sum(gathered) * scale + EPSILON)
        multiply = inverse

        def act(values):
            u = (values - center) * multiply * gain + shift
            return u / (1.0 + jnp.exp(-u))

        for h in range(2):
            value = act(full[h * HM : (h + 1) * HM, :])
            at = W + h * HM
            taps[1, at : at + HM, :] = value
            taps[0, at + 1 : at + 1 + HM, :] = value
            taps[2, at - 1 : at - 1 + HM, :] = value
        for at, rows, raw_left, raw_right in rims:
            from_left = jnp.where(t > 0, act(raw_left), 0.0)
            from_right = jnp.where(t < T - 1, act(raw_right), 0.0)
            taps[0, pl.ds(at, rows, stride=W), :] = from_left
            taps[2, pl.ds(at + W - 1, rows, stride=W), :] = from_right
        zero = jnp.zeros((W, LANES), F32)
        tail = jnp.zeros((taps.shape[1] - W - M, LANES), F32)
        for b in range(3):
            taps[b, 0:W, :] = zero
            taps[b, W + M :, :] = tail

    def first_remote():
        parts = []
        rims = []
        for dt in range(1, T):
            peer = lax.rem(t + dt, T)
            for j in range(S):
                rim_copy(dt, j, False).wait_recv()
                parts.append(
                    (
                        rim_in[peer, j, 2 * RE : 2 * RE + 1, :],
                        rim_in[peer, j, 2 * RE + 1 : 2 * RE + 2, :],
                        TILE,
                    )
                )
        for j in range(S):
            rims.append(
                (W + j * TILE, R, rim_in[left, j, RE : RE + R, :], rim_in[right, j, 0:R, :])
            )
        return parts, rims

    def later_remote(k, incoming):
        for copy in incoming:
            copy.wait_recv()
        parts = []
        rims = []
        for dt in range(1, T):
            peer = lax.rem(t + dt, T)
            for cc in range(C):
                parts.append(
                    (
                        msg_in[k, peer, cc, 2 * pad_edge : 2 * pad_edge + 1, :],
                        msg_in[k, peer, cc, 2 * pad_edge + 1 : 2 * pad_edge + 2, :],
                        HM,
                    )
                )
        for h in range(C):
            rims.append(
                (
                    W + h * HM,
                    HR,
                    msg_in[k, left, h, pad_edge : pad_edge + edge, :],
                    msg_in[k, right, h, 0:edge, :],
                )
            )
        return parts, rims

    def operand(start, rows):
        pairs = []
        for a in range(3):
            for b in range(3):
                pairs.append(split_pair(taps[b, start + a * W : start + a * W + rows, :]))
        return jnp.concatenate(
            [v for pair in pairs for v in pair] + [pair[0] for pair in pairs], axis=1
        )

    def piece_copy(k, i, h):
        block = c * BH + i
        return block, pltpu.make_async_remote_copy(
            src_ref=piece.at[k, i, h],
            dst_ref=piece_in.at[k, s],
            send_sem=p_ssem.at[k, i, h],
            recv_sem=p_rsem.at[k, s],
            device_id={"space": block, "chan": h},
            device_id_type=MESH,
        )

    def conv_send(k, mat):
        for h in range(2):
            part = jnp.dot(operand(h * HM, HM), mat[...], preferred_element_type=F32)
            for i in range(BH):
                pack(piece.at[k, i, h], part[:, i * LANES : (i + 1) * LANES], PM)
                block, copy = piece_copy(k, i, h)
                away = jnp.logical_or(block != s, c != h)

                @pl.when(away)
                def _():
                    copy.start()

                @pl.when(jnp.logical_not(away))
                def _():
                    piece_in[k, s] = piece[k, i, h]

    def conv_receive(k, full, extra):
        holder = s // BH
        for step in range(S):
            source = lax.rem(s + step, S)
            arrival = pltpu.make_async_remote_copy(
                src_ref=piece.at[k, 0, 0],
                dst_ref=piece_in.at[k, source],
                send_sem=p_ssem.at[k, 0, 0],
                recv_sem=p_rsem.at[k, source],
                device_id={"space": source, "chan": holder},
                device_id_type=MESH,
            )
            if step == 0:

                @pl.when(holder != c)
                def _():
                    arrival.wait_recv()

            else:
                arrival.wait_recv()
        total = piece_in[k, 0]
        for j in range(1, S):
            total = total + piece_in[k, j]
        at = 0
        for value in unpack(total, HM):
            rows = pl.ds(pl.multiple_of(c * HM + at, 8), value.shape[0])
            full[rows, :] = value if extra is None else value + extra[rows, :]
            at += value.shape[0]

    def conv_drain(k):
        for h in range(2):
            for i in range(BH):
                block, copy = piece_copy(k, i, h)

                @pl.when(jnp.logical_or(block != s, c != h))
                def _():
                    copy.wait_send()

    for load in loads[1:4]:
        load.wait()
    prepare(w1_raw, w1_mat)
    for step in range(1, S):
        a_copy(step, False).wait_recv()
        a_forward(step, c).start()
    for step in range(1, S):
        a_forward(step, other).wait_recv()
        source = lax.rem(s + step, S)
        at = 0
        for value in unpack(a_in[source], TILE):
            start = pl.multiple_of(source * TILE + at, 8)
            feat_all[pl.ds(start, value.shape[0]), :] = value
            at += value.shape[0]
    parts, rims = first_remote()
    activate(feat_all, parts, rims, pick_block(gain1), pick_block(shift1))
    conv_send(0, w1_mat)

    for load in loads[4:]:
        load.wait()
    prepare(w2_raw, w2_mat)
    blank = jnp.zeros((LANES - 3 * ZH, LANES), F32)
    for b in range(3):
        rows = [padded(head_w[a * 3 + b], LANES) for a in range(3)] + [blank]
        high, low = split_pair(jnp.concatenate(rows, axis=0))
        for place, value in ((3 * b, high), (3 * b + 1, high), (3 * b + 2, low)):
            wh_mat[:, place * LANES : (place + 1) * LANES] = value
    for first, mat in ((0, wn_mat), (4 * (Z + 4), wc_mat)):
        for b in range(2):
            for a in range(2):
                at = (b * 2 + a) * Z
                for n in range(strips):
                    high, low = split_pair(pw_raw[n, pl.ds(first + a * 2 + b, Z, stride=4), :])
                    lanes = slice(n * LANES, (n + 1) * LANES)
                    mat[at : at + Z, lanes] = high
                    mat[4 * Z + at : 4 * Z + at + Z, lanes] = high
                    mat[8 * Z + at : 8 * Z + at + Z, lanes] = low
    mark_sum = jnp.concatenate(
        [
            jnp.sum(pw_raw[n, 4 * Z : 4 * (Z + 4), :], axis=0, keepdims=True)
            for n in range(strips)
        ],
        axis=1,
    )

    PR, PC, PP = dims["PR"], dims["PC"], dims["PP"]
    FULLW = W * T
    cells[...] = jnp.zeros(cells.shape, F32)
    patch[...] = jnp.zeros(patch.shape, F32)

    def build_patches():
        turned[...] = cells[...].T
        for b in range(2):
            picked = turned[pl.ds(b, PC, stride=2), :]
            for p in range(PR):
                patch[p * PP : p * PP + PC, b * 2 * Z : (b + 1) * 2 * Z] = picked[
                    :, p * 2 * Z : (p + 1) * 2 * Z
                ]

    for f in range(FR):
        for i in range(R):
            cells[i * Z : (i + 1) * Z, 0:FULLW] = noisy[f, i]
        build_patches()
        got = jnp.dot(split_columns(patch[:, 0 : 4 * Z]), wn_mat[...], preferred_element_type=F32)
        opening = (t * FR + f) == 0
        base[f] = got + patch_b[...].reshape(1, -1) + jnp.where(opening, mark_sum, 0.0)

    stores = [
        pltpu.make_async_copy(base, base_out, load_sem.at[len(early) + strips]),
        pltpu.make_async_copy(wc_mat, wc_out, load_sem.at[len(early) + strips + 1]),
    ]
    for store in stores:
        store.start()

    conv_receive(0, conv_all.at[0], None)
    sib1 = sibling(0, conv_all.at[0], c)
    sib1.start()
    out2, in2 = exchange(0, conv_all.at[0])
    sibling(0, conv_all.at[0], other).wait_recv()
    parts, rims = later_remote(0, in2)
    activate(conv_all.at[0], parts, rims, pick_block(gain2), pick_block(shift2))
    conv_send(1, w2_mat)

    conv_receive(1, conv_all.at[1], feat_all)
    sib2 = sibling(1, conv_all.at[1], c)
    sib2.start()
    out3, in3 = exchange(1, conv_all.at[1])
    sibling(1, conv_all.at[1], other).wait_recv()
    parts, rims = later_remote(1, in3)
    activate(conv_all.at[1], parts, rims, pick_block(gain3), pick_block(shift3))

    def lat_copy(dest_s, dest_t, dest_c, slot_s, slot_t, slot_c):
        return pltpu.make_async_remote_copy(
            src_ref=lat_send.at[dest_s],
            dst_ref=lat_in.at[slot_t, slot_c, slot_s],
            send_sem=l_ssem.at[dest_t, dest_c, dest_s],
            recv_sem=l_rsem.at[slot_t, slot_c, slot_s],
            device_id={"space": dest_s, "tm": dest_t, "chan": dest_c},
            device_id_type=MESH,
        )

    bias_row = jnp.broadcast_to(head_b[...].reshape(1, ZH), (ZH, ZH))
    diagonal = lax.broadcasted_iota(jnp.int32, (ZH, ZH), 0) == lax.broadcasted_iota(
        jnp.int32, (ZH, ZH), 1
    )
    bias = jnp.sum(jnp.where(diagonal & (s == 0), bias_row, 0.0), axis=1, keepdims=True)
    columns = []
    for b in range(3):
        high, low = split_pair(taps[b, 0 : mixed.shape[0], :])
        columns += [high, low, high]
    mixed[...] = lax.dot_general(
        jnp.concatenate(columns, axis=1),
        wh_mat[...],
        (((1,), (1,)), ((), ())),
        preferred_element_type=F32,
    )
    for j in range(S):
        shifted = [mixed[j * TILE + a * W : j * TILE + a * W + LANES, :] for a in range(3)]
        joined = jnp.where(
            col_id < ZH, shifted[0], jnp.where(col_id < 2 * ZH, shifted[1], shifted[2])
        ).T
        lat_send[j] = joined[0:ZH] + joined[ZH : 2 * ZH] + joined[2 * ZH : 3 * ZH] + bias
    lat_in[t, c, s] = lat_send[s]
    lat_out = []
    lat_arrive = []
    for ds in reversed(range(S)):
        for dt in range(T):
            for dc in range(C):
                if ds or dt or dc:
                    ps = lax.rem(s + ds, S)
                    pt = lax.rem(t + dt, T)
                    pc = lax.rem(c + dc, C)
                    copy = lat_copy(ps, pt, pc, s, t, c)
                    copy.start()
                    lat_out.append(copy)
                    lat_arrive.append(lat_copy(ps, pt, pc, ps, pt, pc))

    conv_drain(0)
    conv_drain(1)
    for copy in out2 + out3 + [sib1, sib2]:
        copy.wait_send()
    for step in range(1, S):
        a_copy(step, True).wait_send()
        a_forward(step, c).wait_send()
    for dt in range(1, T):
        for j in range(S):
            rim_copy(dt, j, True).wait_send()

    for copy in lat_arrive:
        copy.wait_recv()

    def half_latent(tt, cc):
        total = lat_in[tt, cc, 0]
        for j in range(1, S):
            total = total + lat_in[tt, cc, j]
        return total

    for cc in range(C):
        value = half_latent(t, cc)
        for r in range(R):
            latent[r, cc * ZH : (cc + 1) * ZH, :] = value[:, r * W : (r + 1) * W]
    for f in range(FR):
        cells[...] = jnp.zeros(cells.shape, F32)
        opening = (t * FR + f) == 0
        for tt in range(T):
            for cc in range(C):
                value = half_latent(tt, cc)
                for i in range(R):
                    at = i * Z + cc * ZH
                    cells[at : at + ZH, tt * W : (tt + 1) * W] = value[:, i * W : (i + 1) * W]
        for i in range(R):
            rows = slice(i * Z, (i + 1) * Z)
            cells[rows, 0:FULLW] = jnp.where(opening, cells[rows, 0:FULLW], later[f, i])
        build_patches()
        patch_out[f] = patch[...]
    for store in stores:
        store.wait()
    for copy in lat_out:
        copy.wait_send()


def up(value, unit):
    return -(-value // unit) * unit


def packed_rows(rows, width, unit):
    free = LANES - width
    if free <= 0 or width % free or rows % 8:
        return rows
    main = up(-(-rows * width // LANES), unit)
    fits = main < rows and (rows - main) * (width // free) <= main
    return main if fits else rows


def plan(mesh_shape, features, noisy_latents, patch_weight):
    S, T, C = mesh_shape["space"], mesh_shape["tm"], mesh_shape["chan"]
    R, W, CH = features.shape
    FR, Z = noisy_latents.shape[:2]
    dims = dict(S=S, T=T, C=C, R=R, W=W, CH=CH, Z=Z, FR=FR)
    H = S * R
    dims["EDGE"] = up(H // 2, 8)
    dims["PR"], dims["PC"] = R // 2, W * T // 2
    dims["PP"] = up(W * T // 2, 8)
    dims["N"] = patch_weight.shape[1]
    CB = CH // S
    dims["AM"], dims["PM"] = packed_rows(R * W, CB, 16), packed_rows(H * W // 2, CB, 8)
    dims["RE"] = up(R, 8)
    fits = (
        C == 2
        and T > 1
        and S % C == 0
        and CH % S == 0
        and CH // S <= LANES
        and (CH // S) % (CH // NGROUP) == 0
        and (R * W) % 8 == 0
        and (H * W // 2) % 8 == 0
        and H % 2 == 0
        and dims["AM"] % 16 == 0
        and dims["PM"] % 8 == 0
        and R * W <= LANES
        and R * Z <= LANES
        and W * T <= LANES
        and 4 * Z <= LANES
        and dims["N"] % LANES == 0
        and H * W * LANES * 4 <= 2**19
    )
    return dims if fits else None


def fused(dims, args):
    S, T, C = dims["S"], dims["T"], dims["C"]
    R, W, CH = dims["R"], dims["W"], dims["CH"]
    Z, FR, N, EDGE = dims["Z"], dims["FR"], dims["N"], dims["EDGE"]
    CB, NH = CH // S, CH // C
    BH = NH // CB
    M = S * R * W
    MR = 2 * EDGE + 8
    (f, g1, s1, w1, g2, s2, w2, g3, s3, hw, hb, noisy, later, pw, pb) = args
    flat = lambda v: v.reshape((9,) + v.shape[2:])
    by_row = lambda v: jnp.transpose(v, (0, 2, 1, 3))
    operands = (
        f, g1, s1, flat(w1), g2, s2, flat(w2), g3, s3,
        flat(jnp.transpose(hw, (0, 1, 3, 2))), hb, by_row(noisy), by_row(later), pw, pb,
    )
    vmem = pl.BlockSpec(memory_space=pltpu.VMEM)
    in_specs = [pl.BlockSpec(memory_space=pl.ANY)] * 15
    dma = pltpu.SemaphoreType.DMA
    big = lambda n: pltpu.VMEM((27 * LANES, n), BF16)
    scratch = [
        pltpu.VMEM(operands[k].shape, F32) for k in (0, 1, 2, 4, 5, 7, 8, 9, 10, 11, 12, 14)
    ] + [
        pltpu.VMEM((9, CB, NH), F32),
        pltpu.VMEM((9, CB, NH), F32),
        pltpu.VMEM((N // LANES, pw.shape[0], LANES), F32),
        big(BH * LANES),
        big(BH * LANES),
        pltpu.VMEM((LANES, 9 * LANES), BF16),
        pltpu.VMEM((up((S - 1) * R * W + 2 * W + LANES, 16), LANES), F32),
        pltpu.VMEM((12 * Z, N), BF16),
        pltpu.VMEM((12 * Z, N), BF16),
        pltpu.VMEM((FR, dims["PR"] * dims["PP"], N), F32),
        pltpu.VMEM((S, R * W, LANES), F32),
        pltpu.VMEM((S, dims["AM"], LANES), F32),
        pltpu.VMEM((S, dims["AM"], LANES), F32),
        pltpu.VMEM((S, 2 * dims["RE"] + 8, LANES), F32),
        pltpu.VMEM((T, S, 2 * dims["RE"] + 8, LANES), F32),
        pltpu.VMEM((M, LANES), F32),
        pltpu.VMEM((2, M, LANES), F32),
        pltpu.VMEM((3, up(M + 2 * W + LANES, 8), LANES), F32),
        pltpu.VMEM((2, MR, LANES), F32),
        pltpu.VMEM((2, T, C, MR, LANES), F32),
        pltpu.VMEM((2, BH, 2, dims["PM"], LANES), F32),
        pltpu.VMEM((2, S, dims["PM"], LANES), F32),
        pltpu.VMEM((S, Z // C, LANES), F32),
        pltpu.VMEM((T, C, S, Z // C, LANES), F32),
        pltpu.VMEM((LANES, LANES), F32),
        pltpu.VMEM((LANES, LANES), F32),
        pltpu.VMEM((dims["PR"] * dims["PP"], LANES), F32),
        dma((16 + N // LANES,)),
        dma((S,)),
        dma((S,)),
        dma((S,)),
        dma((S,)),
        dma((T, S)),
        dma((T, S)),
        dma((2, T, C)),
        dma((2, T, C)),
        dma((2,)),
        dma((2,)),
        dma((2, BH, 2)),
        dma((2, S)),
        dma((T, C, S)),
        dma((T, C, S)),
    ]
    PR, PC, PP = dims["PR"], dims["PC"], dims["PP"]
    far = pl.BlockSpec(memory_space=pl.ANY)
    patch, base, wc, latent = pl.pallas_call(
        functools.partial(fused_kernel, dims),
        out_shape=(
            jax.ShapeDtypeStruct((FR, PR * PP, LANES), F32),
            jax.ShapeDtypeStruct((FR, PR * PP, N), F32),
            jax.ShapeDtypeStruct((12 * Z, N), BF16),
            jax.ShapeDtypeStruct((R, Z, W), F32),
        ),
        in_specs=in_specs,
        out_specs=(vmem, far, far, vmem),
        scratch_shapes=scratch,
        compiler_params=pltpu.CompilerParams(
            collective_id=0, has_side_effects=True, vmem_limit_bytes=60 * 2**20
        ),
        name="fused_block",
    )(*operands)
    NB = N // 4 if N % (4 * LANES) == 0 else N
    whole = lambda shape: pl.BlockSpec(shape, lambda n: (0,) * len(shape))
    tokens, latent = pl.pallas_call(
        functools.partial(finish_kernel, dims),
        grid=(N // NB,),
        out_shape=(
            jax.ShapeDtypeStruct((PR, PC, FR, N), F32),
            jax.ShapeDtypeStruct((R, Z, W), F32),
        ),
        in_specs=[
            whole((FR, PR * PP, LANES)),
            pl.BlockSpec((FR, PR * PP, NB), lambda n: (0, 0, n)),
            pl.BlockSpec((12 * Z, NB), lambda n: (0, n)),
            whole((R, Z, W)),
        ],
        out_specs=(pl.BlockSpec((PR, PC, FR, NB), lambda n: (0, 0, 0, n)), whole((R, Z, W))),
        name="finish_tokens",
    )(patch, base, wc, latent)
    return jnp.transpose(tokens, (2, 0, 1, 3)), jnp.transpose(latent, (0, 2, 1))


def solution(mesh):
    shape = dict(mesh.shape)

    def step(*args):
        dims = plan(shape, args[0], args[11], args[13])
        return on_device(*args) if dims is None else fused(dims, args)

    return jax.shard_map(
        step,
        mesh=mesh,
        in_specs=(
            P(("groups", "space"), "tm", None),
            P(),
            P(),
            P(None, None, "space", "chan"),
            P(),
            P(),
            P(None, None, "space", "chan"),
            P(),
            P(),
            P(None, None, "space", "chan"),
            P("chan"),
            P(("groups", "tm"), None, "space", None),
            P(("groups", "tm"), None, "space", None),
            P(None, "chan"),
            P("chan"),
        ),
        out_specs=(P(("groups", "tm"), "space", None, "chan"), P(("groups", "space"), "tm", None)),
        check_vma=False,
    )
```

profile of v0, /device:TPU:0, one launch (start us, length us, event | category | flops | bytes accessed | tf_op | source)
XLA Modules:
  0.0 51.7 jit_solution(2974381320475349495)
XLA Ops:
  0.6 47.1 %fused_block.1 = (f32[1,72,128]{2,1,0:T(8,128)}, f32[1,72,2560]{2,1,0:T(8,128)}, bf16[192,2560]{1,0:T(8,128)(2,1)}, f32[6,16,20]{2,1,0:T(8,128)}) custom-call(f32[6,20,384]{2,1,0:T(8,128)} %feat_hbm.1, f32[384]{0:T(512)} %gain1_hbm.1, f32[384]{0:T(512)} %shift1_hbm.1, f32[9,96,192]{2,1,0:T(8,128)} %bitcast.9, f32[384]{0:T(512)} %gain2_hbm.1, f32[384]{0:T(512)} %shift2_hbm.1, ...), custom_call_target="tpu_custom_call" | custom-call | tf_op jit(solution)/shard_map/fused_block/pallas_call | solution.py:927
  47.8 4.0 %finish_tokens.1 = (f32[3,20,1,2560]{3,2,1,0:T(1,128)}, f32[6,16,20]{2,1,0:T(8,128)}) custom-call(f32[1,72,128]{2,1,0:T(8,128)} %get-tuple-element.8.patch, f32[1,72,2560]{2,1,0:T(8,128)} %get-tuple-element.9.base, bf16[192,2560]{1,0:T(8,128)(2,1)} %get-tuple-element.10.wc, f32[6,16,20]{2,1,0:T(8,128)} %get-tuple-element.11.latent_in), custom_call_target="tpu_custom_call" | custom-call | tf_op jit(solution)/shard_map/finish_tokens/pallas_call | solution.py:945
where the time goes:
time: 51.9 us; the launch traced here: 51.7 us
  Pallas kernels  51.1 us (98%)
  between operations  0.64 us (1%)
    pallas_call x1, Pallas kernels, fused(): pl.pallas_call(functools.partial(fused_kernel, dims), out_shape=(jax.Shap...  47.1 us
    pallas_call x1, Pallas kernels, fused(): pl.pallas_call(functools.partial(finish_kernel, dims), grid=(N // NB,), o...  3.96 us

commit v1 on v0

v1 whole, which is shorter than its diff:
```python
import functools
import types

import jax
import jax.numpy as jnp
from jax import lax
from jax.experimental import pallas as pl
from jax.experimental.pallas import tpu as pltpu
from jax.sharding import PartitionSpec as P

NGROUP = 32


EPSILON = 1e-06
HIGHEST = lax.Precision.HIGHEST


def padded_2(cells, sides, width):
    for axis, dim in sides:
        count = lax.axis_size(axis)
        ends = count - 1
        head = lax.slice_in_dim(cells, 0, width, axis=dim)
        tail = lax.slice_in_dim(cells, cells.shape[dim] - width, cells.shape[dim], axis=dim)
        cells = jnp.concatenate(
            [
                lax.ppermute(tail, axis, [(i, (i + 1) % count) for i in range(ends)]),
                cells,
                lax.ppermute(head, axis, [((i + 1) % count, i) for i in range(ends)]),
            ],
            axis=dim,
        )
    return cells


def group_stats(inner, count_all):
    grouped = inner.reshape(-1, NGROUP, inner.shape[-1] // NGROUP)
    totals, squares = lax.psum(
        (jnp.sum(grouped, axis=(0, 2)), jnp.sum(grouped * grouped, axis=(0, 2))), ("space", "tm")
    )
    center = totals / count_all
    spread = squares / count_all - center * center
    return (center, lax.rsqrt(spread + EPSILON))


def normalize_act(values, stats, gain, shift):
    center, inverse = stats
    grouped = values.reshape(values.shape[:-1] + (NGROUP, values.shape[-1] // NGROUP))
    scaled = (grouped - center[:, None]) * inverse[:, None]
    return jax.nn.silu(scaled.reshape(values.shape) * gain + shift)


def tap_columns(padded, rows_out, cols_out):
    shifted = [
        padded[row_tap : row_tap + rows_out, col_tap : col_tap + cols_out, :]
        for row_tap in range(3)
        for col_tap in range(3)
    ]
    return jnp.stack(shifted, axis=2).reshape(rows_out * cols_out, 9, padded.shape[-1])


def add_taps(columns, piece):
    depth = piece.shape[2]
    picked = columns.reshape(columns.shape[0], 9 * depth)
    return jnp.dot(
        picked,
        piece.reshape(9 * depth, piece.shape[3]),
        precision=HIGHEST,
        preferred_element_type=jnp.float32,
    )


def wide_conv(padded, weight, rows_out, cols_out):
    columns = tap_columns(padded, rows_out, cols_out)
    summed = add_taps(columns, lax.all_gather(weight, "space", axis=2, tiled=True))
    return lax.all_gather(summed.reshape(rows_out, cols_out, -1), "chan", axis=2, tiled=True)


def border_rim(values):
    return padded_2(values, (("space", 0), ("tm", 1)), 1)


def on_device(
    features,
    norm1_gain,
    norm1_shift,
    conv1_weight,
    norm2_gain,
    norm2_shift,
    conv2_weight,
    head_gain,
    head_shift,
    head_weight,
    head_bias,
    noisy_latents,
    later_cond,
    patch_weight,
    patch_bias,
):
    tile_rows = features.shape[0]
    tile_cols = features.shape[1]
    count_all = float(
        tile_rows
        * tile_cols
        * lax.axis_size("space")
        * lax.axis_size("tm")
        * (features.shape[2] // NGROUP)
    )
    first_stats = group_stats(features, count_all)
    active = normalize_act(features, first_stats, norm1_gain, norm1_shift)
    first_conv = wide_conv(border_rim(active), conv1_weight, tile_rows, tile_cols)
    second_stats = group_stats(first_conv, count_all)
    second_act = normalize_act(first_conv, second_stats, norm2_gain, norm2_shift)
    second_conv = wide_conv(border_rim(second_act), conv2_weight, tile_rows, tile_cols)
    hidden = features + second_conv
    head_stats = group_stats(hidden, count_all)
    head_act = normalize_act(hidden, head_stats, head_gain, head_shift)
    head_pad = padded_2(head_act, (("space", 0), ("tm", 1)), 1)
    head_columns = tap_columns(head_pad, tile_rows, tile_cols)
    latent_part = (
        add_taps(head_columns, lax.all_gather(head_weight, "space", axis=2, tiled=True)) + head_bias
    )
    image_latent = lax.all_gather(
        latent_part.reshape(tile_rows, tile_cols, -1), "chan", axis=2, tiled=True
    )
    latent_row = lax.all_gather(image_latent, "tm", axis=1, tiled=True)
    frame_count = noisy_latents.shape[0]
    full_width = noisy_latents.shape[3]
    frame_ids = lax.axis_index("tm") * frame_count + jnp.arange(frame_count)
    opening = frame_ids == 0
    condition = jnp.where(
        opening[:, None, None, None], jnp.transpose(latent_row, (2, 0, 1))[None], later_cond
    )
    marks = jnp.broadcast_to(
        opening.astype(jnp.float32)[:, None, None, None], (frame_count, 4, tile_rows, full_width)
    )
    stacked = jnp.concatenate([noisy_latents, marks, condition], axis=1)
    channel_count = stacked.shape[1]
    patches = (
        stacked.reshape(frame_count, channel_count, tile_rows // 2, 2, full_width // 2, 2)
        .transpose(0, 2, 4, 1, 3, 5)
        .reshape(-1, channel_count * 4)
    )
    tokens = (
        jnp.dot(patches, patch_weight, precision=HIGHEST, preferred_element_type=jnp.float32)
        + patch_bias
    )
    return (tokens.reshape(frame_count, tile_rows // 2, full_width // 2, -1), image_latent)


MESH = pl.DeviceIdType.MESH
LANES = 128
BF16 = jnp.bfloat16
F32 = jnp.float32


def split_pair(values):
    high = values.astype(BF16)
    return high, (values - high.astype(F32)).astype(BF16)


def split_columns(values):
    high, low = split_pair(values)
    return jnp.concatenate([high, low, high], axis=1)


def finish_kernel(dims, parts, patch, base, wc, latent_in, tokens, latent, tok, sem):
    PC, PP, Z, FR = dims["PC"], dims["PP"], dims["Z"], dims["FR"]
    width = dims["N"] // parts
    copies = [pltpu.make_async_copy(latent_in, latent, sem.at[parts])]
    copies[0].start()
    lhs = [split_columns(patch[f, :, 0 : 4 * Z]) for f in range(FR)]
    for n in range(parts):
        lanes = slice(n * width, (n + 1) * width)
        for f in range(FR):
            got = base[f, :, lanes] + jnp.dot(lhs[f], wc[:, lanes], preferred_element_type=F32)
            for p in range(dims["PR"]):
                tok[p, :, f, lanes] = got[p * PP : p * PP + PC, :]
        view = (slice(None), slice(None), slice(None), pl.ds(n * width, width))
        copies.append(pltpu.make_async_copy(tok.at[view], tokens.at[view], sem.at[n]))
        copies[-1].start()
    for copy in copies:
        copy.wait()


def fused_kernel(dims, names, *refs):
    S, T, C = dims["S"], dims["T"], dims["C"]
    R, W, CH = dims["R"], dims["W"], dims["CH"]
    Z, FR = dims["Z"], dims["FR"]
    CB = CH // S
    TILE = R * W
    REG = 2 * TILE
    per_group = CH // NGROUP
    ZH = Z // C
    AM, PM, WQ, WM = dims["AM"], dims["PM"], dims["WQ"], dims["WM"]
    QR = CB // 4
    AT = 8
    LAST = 2 * R + 1
    MR = up(2 * R + 2, 8)
    (
        feat_hbm, gain1_hbm, shift1_hbm, w1_hbm, gain2_hbm, shift2_hbm, w2_hbm, gain3_hbm,
        shift3_hbm, head_w_hbm, head_b_hbm, noisy_hbm, later_hbm, pw_hbm, patch_b_hbm,
    ) = refs[:15]
    patch_out, base_out, wc_out, latent = refs[15:19]
    v = types.SimpleNamespace(**dict(zip(names, refs[19:])))
    s = lax.axis_index("space")
    t = lax.axis_index("tm")
    c = lax.axis_index("chan")
    g = lax.axis_index("groups")
    p, hh = lax.rem(s, 2), lax.div(s, 2)
    pair, far, far2 = s + 1 - 2 * p, lax.rem(s + 2, 4), 3 - s
    tx, oc, gy = 1 - t, 1 - c, 1 - g
    inner = (p + hh) == 1
    own, side = 2 * t + p, 2 * tx + p
    near, cross = 2 * t + 1 - p, 2 * tx + 1 - p
    home = c == t
    stray = c != t
    sent = []

    def remote(src, dst, ssem, rsem, **where):
        return pltpu.make_async_remote_copy(
            src_ref=src, dst_ref=dst, send_sem=ssem, recv_sem=rsem, device_id=where,
            device_id_type=MESH,
        )

    def go(copy):
        copy.start()
        sent.append((None, copy))

    def go_if(condition, copy):
        @pl.when(condition)
        def _():
            copy.start()

        sent.append((condition, copy))

    early = (
        (feat_hbm, v.feat), (w1_hbm, v.w1_raw), (gain1_hbm, v.gain1), (shift1_hbm, v.shift1),
        (w2_hbm, v.w2_raw), (gain2_hbm, v.gain2), (shift2_hbm, v.shift2),
        (gain3_hbm, v.gain3), (shift3_hbm, v.shift3), (head_w_hbm, v.head_w),
        (head_b_hbm, v.head_b), (noisy_hbm, v.noisy), (later_hbm, v.later),
        (patch_b_hbm, v.patch_b),
    )
    loads = [
        pltpu.make_async_copy(src, dst, v.load_sem.at[k]) for k, (src, dst) in enumerate(early)
    ]
    strips = v.pw_raw.shape[0]
    loads += [
        pltpu.make_async_copy(
            pw_hbm.at[:, n * LANES : (n + 1) * LANES], v.pw_raw.at[n], v.load_sem.at[len(early) + n]
        )
        for n in range(strips)
    ]
    for load in loads:
        load.start()

    v.lat_in[...] = jnp.zeros(v.lat_in.shape, F32)
    barrier = pltpu.get_barrier_semaphore()
    for ds in range(S):
        for dt in range(T):
            for dc in range(C):
                if ds or dt or dc:
                    pl.semaphore_signal(
                        barrier,
                        inc=1,
                        device_id={
                            "space": lax.rem(s + ds, S),
                            "tm": lax.rem(t + dt, T),
                            "chan": lax.rem(c + dc, C),
                        },
                        device_id_type=MESH,
                    )
    pl.semaphore_signal(barrier, inc=1, device_id={"groups": gy}, device_id_type=MESH)

    def padded(values, width=LANES):
        rows = values.shape[0]
        if width == values.shape[1]:
            return values
        return jnp.concatenate([values, jnp.zeros((rows, width - values.shape[1]), values.dtype)], axis=1)

    def pack(dst, value, main):
        rows = value.shape[0]
        dst[...] = value[0:main]
        rest = rows - main
        free = LANES - CB
        for j in range(CB // free if rest else 0):
            dst[j * rest : (j + 1) * rest, CB:LANES] = value[main:rows, j * free : (j + 1) * free]

    def unpack(value, rows):
        main = value.shape[0]
        rest = rows - main
        if not rest:
            return (value,)
        free = LANES - CB
        columns = [value[j * rest : (j + 1) * rest, CB:LANES] for j in range(CB // free)]
        return value, padded(jnp.concatenate(columns, axis=1))

    def channel_stats(values):
        total = jnp.sum(values, axis=0, keepdims=True)
        middle = total * (1.0 / values.shape[0])
        away = values - middle
        return total, jnp.sum(away * away, axis=0, keepdims=True)

    loads[0].wait()
    for r in range(R):
        line = v.feat[r]
        for q in range(S):
            v.tile[q, r * W : (r + 1) * W, :] = padded(line[:, q * CB : (q + 1) * CB])
    own_rows = pl.ds(pl.multiple_of(p * TILE, 8), TILE)
    for q in range(S):
        value = v.tile[q]
        v.feat_all[q, own_rows, :] = value
        pack(v.a_pack.at[q], value, AM)
        total, spread = channel_stats(value)
        v.st[q : q + 1, :] = total
        v.st[S + q : S + q + 1, :] = spread
        edge = jnp.where(
            t == 0, v.tile[q, pl.ds(W - 1, R, stride=W), :], v.tile[q, pl.ds(0, R, stride=W), :]
        )
        v.colf[q, 0:R, :] = edge
        v.rowf[q, 0:W, :] = jnp.where(hh == 0, value[TILE - W : TILE], value[0:W])
        v.corf[q : q + 1, :] = jnp.where(hh == 0, edge[R - 1 : R], edge[0:1])
    v.st_in[t, s] = v.st[...]

    @pl.when(stray)
    def _():
        v.colf_in[p] = v.colf[...]

    def w_pack(k, raw):
        @pl.when(home)
        def _():
            for cc in range(C):
                rows = pl.ds(pl.multiple_of(QR * (2 * g + cc), 8), QR)
                for pp in range(2):
                    pieces = [raw[tap, rows, :][:, pp * CB : (pp + 1) * CB] for tap in range(9)]
                    pack(v.wpack.at[k, pp, cc], padded(jnp.concatenate(pieces, axis=0)), WM)

    loads[1].wait()
    w_pack(0, v.w1_raw)

    def w_own(k, raw):
        @pl.when(home)
        def _():
            for tap in range(9):
                w = raw[tap]
                v.wown[k, tap * CB : (tap + 1) * CB, :] = padded(
                    jnp.where(p == 0, w[:, 0:CB], w[:, CB : 2 * CB])
                )

    w_own(0, v.w1_raw)

    row_id = lax.broadcasted_iota(jnp.int32, (LANES, LANES), 0)
    col_id = lax.broadcasted_iota(jnp.int32, (LANES, LANES), 1)
    same = ((row_id // per_group) == (col_id // per_group)) & (row_id < CB) & (col_id < CB)
    member = jnp.where(same, 1.0, 0.0).astype(F32)

    def group_sum(rows8):
        return jnp.dot(rows8, member, precision=HIGHEST, preferred_element_type=F32)

    def store_mat(k, q, tap, w):
        high, low = split_pair(w)
        v.mat[k, q, tap * LANES : tap * LANES + CB, 0:LANES] = high
        v.mat[k, q, tap * LANES : tap * LANES + CB, LANES : 2 * LANES] = low

    def own_copy(k):
        return remote(v.wown.at[k], v.wown.at[k], v.es.at[k], v.er.at[k], chan=oc)

    def own_mat(k):
        pl.when(stray)(own_copy(k).wait_recv)
        for tap in range(9):
            store_mat(k, s, tap, v.wown[k, tap * CB : (tap + 1) * CB, :])

    gap = jnp.zeros((LANES - CB, 2 * LANES), BF16)
    for k in range(2):
        for q in range(S):
            for tap in range(9):
                v.mat[k, q, tap * LANES + CB : (tap + 1) * LANES, :] = gap

    def z_copy(k, peer, slot, cc):
        return remote(
            v.wpack.at[k, lax.rem(peer, 2), cc], v.wq.at[k, slot, 2 * g + cc],
            v.zs.at[k, peer, cc], v.zr.at[k, slot], space=peer, chan=cc,
        )

    def y_copy(k, z, which):
        ref = v.wq.at[k, z, which]
        return remote(ref, ref, v.ys.at[k, z], v.yr.at[k, z], groups=gy)

    def b_copy(k, z, which, n):
        ref = v.wq.at[k, z, which]
        return remote(ref, ref, v.bs.at[k, z, n], v.br.at[k, z, n], chan=oc)

    order = (far, far2, pair)

    def z_send(k, z):
        for cc in range(C):
            go_if(home, z_copy(k, z, s, cc))

    def relay(k, z):
        remote(
            v.wpack.at[k, 0, 0], v.wq.at[k, z, 2 * g + c], v.zs.at[k, z, 0], v.zr.at[k, z],
            space=z, chan=t,
        ).wait_recv()
        go(y_copy(k, z, 2 * g + c))
        go(b_copy(k, z, 2 * g + c, 0))

    def relay2(k, z):
        y_copy(k, z, 2 * gy + c).wait_recv()
        go(b_copy(k, z, 2 * gy + c, 1))

    def finish_weights(k, z):
        b_copy(k, z, 2 * g + oc, 0).wait_recv()
        b_copy(k, z, 2 * gy + oc, 1).wait_recv()
        for kk in range(4):
            at = 0
            for value in unpack(v.wq[k, z, kk], WQ):
                for n in range(value.shape[0] // 8):
                    tap, off = divmod(at, QR)
                    to = tap * CB + kk * QR + off
                    v.wf[to : to + 8, :] = value[n * 8 : n * 8 + 8]
                    at += 8
        for tap in range(9):
            store_mat(k, z, tap, v.wf[tap * CB : (tap + 1) * CB, :])

    pl.semaphore_wait(barrier, S * T * C)

    def feat_copy(n, slot, **where):
        return remote(v.a_pack, v.a_in.at[slot], v.as_sem.at[n], v.ar_sem.at[slot], **where)

    def feat_part(m):
        blocks = pl.ds(2 * m, 2)
        return remote(
            v.a_pack.at[blocks], v.a_in.at[p, blocks], v.fs.at[m], v.fr.at[m], space=pair
        )

    def st_copy(dt, peer, mt, ms):
        return remote(
            v.st, v.st_in.at[mt, ms], v.ss_sem.at[dt, peer], v.sr_sem.at[mt, ms],
            space=peer, tm=tx if dt else t,
        )

    def col_copy(n, slot, **where):
        return remote(v.colf, v.colf_in.at[slot], v.cs_sem.at[n], v.cr_sem.at[slot], **where)

    hub = inner & home
    row_copy = remote(v.rowf, v.rowf_in, v.rs_sem.at[0], v.rr_sem.at[0], space=far2)

    def row_forward(n, **where):
        return remote(v.rowf_in, v.rowf_in, v.rs_sem.at[1 + n], v.rr_sem.at[1], **where)

    def cor_copy(n, **where):
        return remote(v.corf, v.corf_in, v.os_sem.at[n], v.or_sem.at[0], **where)

    st_peers = [(0, far), (0, far2), (1, far), (1, far2), (0, pair), (1, pair), (1, s)]
    go_if(hub, row_copy)
    for dt, peer in st_peers:
        go(st_copy(dt, peer, t, s))
    for n, (peer, column) in enumerate(((far, t), (far2, t), (far, tx), (far2, tx))):
        go_if(inner & stray, cor_copy(n, space=peer, tm=column))
    go_if(stray, col_copy(0, p, tm=tx))
    go_if(stray, col_copy(1, p, space=pair))
    go_if(stray, col_copy(2, p, space=pair, tm=tx))
    go_if(home, feat_part(0))
    go_if(home, feat_part(1))
    go_if(home, feat_copy(0, p, tm=tx))
    z_send(0, far)
    go_if(home, own_copy(0))
    z_send(0, far2)
    bias_copy = remote(v.bias_out, v.bias_in, v.is_sem.at[0], v.ir_sem.at[0], chan=oc)

    for load in loads[2:]:
        load.wait()
    for n, (gain, shift) in enumerate(
        ((v.gain1, v.shift1), (v.gain2, v.shift2), (v.gain3, v.shift3))
    ):
        for j, ref in enumerate((gain, shift)):
            row = ref[...].reshape(1, CH)
            for q in range(S):
                v.prm[n, q, j : j + 1, :] = padded(row[:, q * CB : (q + 1) * CB])
    bias_row = jnp.broadcast_to(v.head_b[...].reshape(1, ZH), (ZH, ZH))
    diagonal = lax.broadcasted_iota(jnp.int32, (ZH, ZH), 0) == lax.broadcasted_iota(
        jnp.int32, (ZH, ZH), 1
    )
    my_bias = jnp.sum(jnp.where(diagonal, bias_row, 0.0), axis=1, keepdims=True)
    v.bias_out[...] = jnp.broadcast_to(my_bias, (ZH, LANES))
    go(bias_copy)
    own_mat(0)
    for tap in range(9):
        v.hw_send[tap] = padded(v.head_w[tap])

    @pl.when(hub)
    def _():
        row_copy.wait_recv()

    for n, where in enumerate((dict(space=pair), dict(tm=tx), dict(space=pair, tm=tx))):
        go_if(hub, row_forward(n, **where))
    z_send(0, pair)
    w_pack(1, v.w2_raw)
    w_own(1, v.w2_raw)
    go_if(home, own_copy(1))
    def feat_pass(m):
        ref = v.a_in.at[1 - p, pl.ds(2 * m, 2)]
        return remote(ref, ref, v.gs.at[m], v.fr.at[m], tm=tx)

    relay(0, far)
    for m in range(2):
        pl.when(home)(feat_part(m).wait_recv)
        go_if(home, feat_pass(m))

    def hw_copy(n, slot, **where):
        return remote(v.hw_send, v.hwq.at[slot], v.hs.at[n], v.hr.at[slot], **where)

    @pl.when(hh == t)
    def _():
        v.hwq[c] = v.hw_send[...]

    def unpack_features(slot):
        for q in range(S):
            at = 0
            for value in unpack(v.a_in[slot, q], TILE):
                rows = pl.ds(pl.multiple_of(slot * TILE + at, 8), value.shape[0])
                v.feat_all[q, rows, :] = value
                at += value.shape[0]

    @pl.when(stray)
    def _():
        feat_copy(0, p, tm=tx).wait_recv()
        unpack_features(p)

    @pl.when(stray)
    def _():
        for m in range(2):
            feat_pass(m).wait_recv()

    unpack_features(1 - p)
    for dt, peer in st_peers:
        st_copy(dt, peer, tx if dt else t, peer).wait_recv()
    col_copy(1, 1 - p, space=pair).wait_recv()
    pl.when(home)(col_copy(0, p, tm=tx).wait_recv)
    cor_copy(0, space=far).wait_recv()
    pl.when(jnp.logical_not(hub))(row_forward(0, space=pair).wait_recv)

    for z in order:
        z_send(1, z)
    scale = 1.0 / float(per_group * TILE * S * T)
    everyone = [v.st_in[tt, ss] for tt in range(T) for ss in range(S)]
    total8 = everyone[0]
    for part in everyone[1:]:
        total8 = total8 + part
    summed = group_sum(total8)
    center8 = summed * scale
    gathered = jnp.zeros((8, LANES), F32)
    for part in everyone:
        away = part * (1.0 / TILE) - center8
        gathered = gathered + away * away * float(TILE)
    inverse4 = lax.rsqrt((group_sum(gathered)[0:S] + summed[S : 2 * S]) * scale + EPSILON)

    def build_taps(n, q, value, columns, corner, row, center, inverse):
        gain, shift = v.prm[n, q, 0:1, :], v.prm[n, q, 1:2, :]

        def act(values):
            u = (values - center) * inverse * gain + shift
            return u / (1.0 + jnp.exp(-u))

        inside = act(value)
        line = act(row)
        top, bottom = jnp.where(hh == 1, line, 0.0), jnp.where(hh == 0, line, 0.0)
        tail = jnp.zeros((8, LANES), F32)
        for b in range(3):
            at = AT + 1 - b
            v.taps[q, b, AT + (LAST + 1) * W : AT + (LAST + 1) * W + 8, :] = tail
            v.taps[q, b, at : at + W, :] = top
            v.taps[q, b, at + W : at + W + REG, :] = inside
            v.taps[q, b, at + W + REG : at + 2 * W + REG, :] = bottom
        tip = act(corner)
        sides = [(0, 1, jnp.where(hh == 1, tip, 0.0)), (LAST, 1, jnp.where(hh == 0, tip, 0.0))]
        sides += [(1 + first, count, act(raw)) for first, count, raw in columns]
        for first, count, piece in sides:
            at = AT + first * W
            from_left = jnp.where(c == 1, piece, 0.0)
            from_right = jnp.where(c == 0, piece, 0.0)
            if count == 1:
                v.taps[q, 0, at : at + 1, :] = from_left
                v.taps[q, 2, at + W - 1 : at + W, :] = from_right
            else:
                v.taps[q, 0, pl.ds(at, count, stride=W), :] = from_left
                v.taps[q, 2, pl.ds(at + W - 1, count, stride=W), :] = from_right

    def first_taps(q):
        build_taps(
            0, q, v.feat_all[q],
            [(0, R, v.colf_in[0, q, 0:R, :]), (R, R, v.colf_in[1, q, 0:R, :])],
            v.corf_in[q : q + 1, :], v.rowf_in[q, 0:W, :],
            center8[q : q + 1], inverse4[q : q + 1],
        )

    def operand(q):
        highs, lows = [], []
        for a in range(3):
            for b in range(3):
                high, low = split_pair(v.taps[q, b, AT + a * W : AT + a * W + REG, :])
                highs.append(high)
                lows.append(low)
        return jnp.concatenate(
            [jnp.concatenate(highs, axis=1), jnp.concatenate(lows, axis=1)], axis=0
        )

    def conv_block(k, q):
        part = jnp.dot(operand(q), v.mat[k, q], preferred_element_type=F32)
        return part[0:REG, 0:LANES] + part[0:REG, LANES:] + part[REG:, 0:LANES]

    for q in range(S):
        first_taps(q)
    relay(0, far2)
    relay2(0, far)
    v.acc[...] = conv_block(0, s)
    relay(0, pair)
    go_if(hh == t, hw_copy(0, c, chan=oc))
    go_if(hh == t, hw_copy(1, c, space=far))
    go_if(hh == t, hw_copy(2, c, space=far, chan=oc))
    relay2(0, far2)
    finish_weights(0, far)
    v.acc[...] += conv_block(0, far)
    relay(1, far)
    relay2(0, pair)
    finish_weights(0, far2)
    v.acc[...] += conv_block(0, far2)
    own_mat(1)
    finish_weights(0, pair)
    first = v.acc[...] + conv_block(0, pair)
    v.conv_raw[own] = first

    def rim_exchange(k, full):
        value = full[...]
        total, spread = channel_stats(value)
        column = jnp.where(
            c == 0, full[pl.ds(W - 1, 2 * R, stride=W), :], full[pl.ds(0, 2 * R, stride=W), :]
        )
        row = jnp.where(hh == 0, value[REG - W : REG], value[0:W])
        corner = jnp.where(hh == 0, column[2 * R - 1 : 2 * R], column[0:1])
        for ref, first, rows in ((v.rowm, W, row), (v.colm, 2 * R, column), (v.corm, 1, corner)):
            ref[k, 0:first, :] = rows
            ref[k, first : first + 1, :] = total
            ref[k, first + 1 : first + 2, :] = spread
        copies = [
            remote(v.corm.at[k], v.corm_in.at[k], v.ks.at[k, 0], v.kr.at[k, 0], space=far, chan=oc),
            remote(v.rowm.at[k], v.rowm_in.at[k], v.ks.at[k, 1], v.kr.at[k, 1], space=far),
            remote(v.colm.at[k], v.colm_in.at[k], v.ks.at[k, 2], v.kr.at[k, 2], chan=oc),
        ]
        for copy in copies:
            go(copy)
        return copies, total, spread

    def rim_finish(k, copies, total, spread):
        for copy in copies:
            copy.wait_recv()
        parts = [(total, spread)]
        for ref, first in ((v.rowm_in, W), (v.colm_in, 2 * R), (v.corm_in, 1)):
            parts.append((ref[k, first : first + 1, :], ref[k, first + 1 : first + 2, :]))
        whole = parts[0][0] + parts[1][0] + parts[2][0] + parts[3][0]
        wide = lambda row: jnp.broadcast_to(row, (8, LANES))
        center = group_sum(wide(whole))[0:1] * scale
        spreads = jnp.zeros((1, LANES), F32)
        for part_total, part_spread in parts:
            away = part_total * (1.0 / REG) - center
            spreads = spreads + part_spread + away * away * float(REG)
        inverse = lax.rsqrt(group_sum(wide(spreads))[0:1] * scale + EPSILON)
        return center, inverse

    rims1 = rim_exchange(0, v.conv_raw.at[own])
    pack(v.ypack, first, PM)
    near_copy = remote(v.ypack, v.yin.at[0], v.vs.at[0], v.vr.at[0], space=pair)
    go(near_copy)
    side_copy = remote(v.ypack, v.yin.at[2], v.vs.at[1], v.vr.at[1], tm=tx)
    go(side_copy)
    cross_copy = remote(v.yin.at[0], v.yin.at[1], v.vs.at[2], v.vr.at[2], tm=tx)
    relay(1, far2)
    relay(1, pair)
    relay2(1, far)
    center, inverse = rim_finish(0, *rims1)
    v.rl_in[own, 0 : 2 * R, :] = v.colm_in[0, 0 : 2 * R, :]
    v.rl_in[own, 2 * R : 2 * R + 1, :] = v.corm_in[0, 0:1, :]
    v.rl_in[own, 2 * R + 1 : 2 * R + 2, :] = center
    v.rl_in[own, 2 * R + 2 : 2 * R + 3, :] = inverse
    v.rl_in[own, MR : MR + W, :] = v.rowm_in[0, 0:W, :]

    def rl_copy(n, q, **where):
        ref = v.rl_in.at[q]
        return remote(ref, ref, v.ls.at[n], v.lr.at[q], **where)

    go(rl_copy(0, own, space=pair))
    go(rl_copy(1, own, space=pair, tm=tx))
    go(rl_copy(2, own, tm=tx))

    def second_taps(q):
        build_taps(
            1, q, v.conv_raw[q], [(0, 2 * R, v.rl_in[q, 0 : 2 * R, :])],
            v.rl_in[q, 2 * R : 2 * R + 1, :], v.rl_in[q, MR : MR + W, :],
            v.rl_in[q, 2 * R + 1 : 2 * R + 2, :], v.rl_in[q, 2 * R + 2 : 2 * R + 3, :],
        )

    second_taps(own)
    relay2(1, far2)
    near_copy.wait_recv()
    go(cross_copy)
    finish_weights(1, far)
    v.acc[...] = conv_block(1, own)

    def unpack_conv(slot, q):
        at = 0
        for value in unpack(v.yin[slot], REG):
            v.conv_raw[q, at : at + value.shape[0], :] = value
            at += value.shape[0]

    side_copy.wait_recv()
    rl_copy(2, side, tm=tx).wait_recv()
    unpack_conv(2, side)
    second_taps(side)
    relay2(1, pair)
    v.acc[...] += conv_block(1, side)
    rl_copy(0, near, space=pair).wait_recv()
    unpack_conv(0, near)
    second_taps(near)
    cross_copy.wait_recv()
    rl_copy(1, cross, space=pair, tm=tx).wait_recv()
    unpack_conv(1, cross)
    second_taps(cross)
    finish_weights(1, far2)
    v.acc[...] += conv_block(1, far2)
    finish_weights(1, pair)
    v.hid[...] = v.acc[...] + conv_block(1, pair) + v.feat_all[own]
    rims2 = rim_exchange(1, v.hid)

    @pl.when(hh == t)
    def _():
        hw_copy(0, oc, chan=oc).wait_recv()

    @pl.when(hh != t)
    def _():
        for slot in range(C):
            hw_copy(1, slot, space=far).wait_recv()

    bias_copy.wait_recv()
    blank = jnp.zeros((LANES - 3 * Z, LANES), F32)
    for b in range(3):
        rows = [v.hwq[cc, a * 3 + b] for a in range(3) for cc in range(C)] + [blank]
        high, low = split_pair(jnp.concatenate(rows, axis=0))
        for place, value in ((3 * b, high), (3 * b + 1, high), (3 * b + 2, low)):
            v.wh_mat[:, place * LANES : (place + 1) * LANES] = value
    ours, other_bias = v.bias_out[...], v.bias_in[...]
    bias = jnp.where(
        own == 0,
        jnp.concatenate(
            [jnp.where(c == cc, ours, other_bias) for cc in range(C)], axis=0
        ),
        0.0,
    )

    for first, mat in ((0, v.wn_mat), (4 * (Z + 4), wc_out)):
        for b in range(2):
            for a in range(2):
                at = (b * 2 + a) * Z
                for n in range(strips):
                    high, low = split_pair(v.pw_raw[n, pl.ds(first + a * 2 + b, Z, stride=4), :])
                    lanes = slice(n * LANES, (n + 1) * LANES)
                    mat[at : at + Z, lanes] = high
                    mat[4 * Z + at : 4 * Z + at + Z, lanes] = high
                    mat[8 * Z + at : 8 * Z + at + Z, lanes] = low
    mark_sum = jnp.concatenate(
        [
            jnp.sum(v.pw_raw[n, 4 * Z : 4 * (Z + 4), :], axis=0, keepdims=True)
            for n in range(strips)
        ],
        axis=1,
    )

    PR, PC, PP = dims["PR"], dims["PC"], dims["PP"]
    FULLW = W * T
    cells, turned, patch = v.cells, v.turned, v.patch
    cells[...] = jnp.zeros(cells.shape, F32)
    patch[...] = jnp.zeros(patch.shape, F32)

    def build_patches():
        turned[...] = cells[...].T
        for b in range(2):
            picked = turned[pl.ds(b, PC, stride=2), :]
            for i in range(PR):
                patch[i * PP : i * PP + PC, b * 2 * Z : (b + 1) * 2 * Z] = picked[
                    :, i * 2 * Z : (i + 1) * 2 * Z
                ]

    for f in range(FR):
        for i in range(R):
            cells[i * Z : (i + 1) * Z, 0:FULLW] = v.noisy[f, i]
        build_patches()
        got = jnp.dot(split_columns(patch[:, 0 : 4 * Z]), v.wn_mat[...], preferred_element_type=F32)
        opening = (t * FR + f) == 0
        base_out[f] = got + v.patch_b[...].reshape(1, -1) + jnp.where(opening, mark_sum, 0.0)

    center, inverse = rim_finish(1, *rims2)
    build_taps(
        2, own, v.hid[...], [(0, 2 * R, v.colm_in[1, 0 : 2 * R, :])], v.corm_in[1, 0:1, :],
        v.rowm_in[1, 0:W, :], center, inverse,
    )

    columns = []
    for b in range(3):
        high, low = split_pair(v.taps[own, b, AT : AT + v.mixed.shape[0], :])
        columns += [high, low, high]
    v.mixed[...] = lax.dot_general(
        jnp.concatenate(columns, axis=1),
        v.wh_mat[...],
        (((1,), (1,)), ((), ())),
        preferred_element_type=F32,
    )
    for j in range(2):
        shifted = [v.mixed[j * TILE + a * W : j * TILE + a * W + LANES, :] for a in range(3)]
        joined = jnp.where(
            col_id < Z, shifted[0], jnp.where(col_id < 2 * Z, shifted[1], shifted[2])
        ).T
        v.lat_send[j] = joined[0:Z] + joined[Z : 2 * Z] + joined[2 * Z : 3 * Z] + bias
    v.lat_in[c, own] = v.lat_send[p]

    def lat_copy(dp, dt, dc, slot_c, slot_q):
        return remote(
            v.lat_send.at[1 - p if dp else p], v.lat_in.at[slot_c, slot_q],
            v.ts.at[dp, dt, dc], v.tr.at[slot_c, slot_q],
            space=pair if dp else s, tm=tx if dt else t, chan=oc if dc else c,
        )

    hops = [(1, 1, 1), (1, 1, 0), (0, 1, 1), (0, 1, 0), (1, 0, 1), (1, 0, 0), (0, 0, 1)]
    for dp, dt, dc in hops:
        go_if(((tx if dt else t) == 0) | (c == 1), lat_copy(dp, dt, dc, c, own))

    for condition, copy in sent:
        if condition is None:
            copy.wait_send()
        else:
            pl.when(condition)(copy.wait_send)

    for dp, dt, dc in hops:
        from_c = oc if dc else c
        source = 2 * (tx if dt else t) + (1 - p if dp else p)
        pl.when((t == 0) | (from_c == 1))(lat_copy(dp, dt, dc, from_c, source).wait_recv)

    def latent_of(tt):
        return v.lat_in[tt, 0] + v.lat_in[tt, 1] + v.lat_in[tt, 2] + v.lat_in[tt, 3]

    value = latent_of(t)
    for r in range(R):
        latent[r] = value[:, r * W : (r + 1) * W]
    for f in range(FR):
        cells[...] = jnp.zeros(cells.shape, F32)
        opening = (t * FR + f) == 0
        for tt in range(T):
            value = latent_of(tt)
            for i in range(R):
                cells[i * Z : (i + 1) * Z, tt * W : (tt + 1) * W] = value[:, i * W : (i + 1) * W]
        for i in range(R):
            rows = slice(i * Z, (i + 1) * Z)
            cells[rows, 0:FULLW] = jnp.where(opening, cells[rows, 0:FULLW], v.later[f, i])
        build_patches()
        patch_out[f] = patch[...]


def up(value, unit):
    return -(-value // unit) * unit


def packed_rows(rows, width, unit):
    free = LANES - width
    if free <= 0 or width % free or rows % 8:
        return rows
    main = up(-(-rows * width // LANES), unit)
    fits = main < rows and (rows - main) * (width // free) <= main
    return main if fits else rows


def plan(mesh_shape, features, noisy_latents, patch_weight, head_weight):
    S, T, C, G = (mesh_shape[axis] for axis in ("space", "tm", "chan", "groups"))
    R, W, CH = features.shape
    FR, Z = noisy_latents.shape[:2]
    dims = dict(S=S, T=T, C=C, R=R, W=W, CH=CH, Z=Z, FR=FR)
    dims["PR"], dims["PC"] = R // 2, W * T // 2
    dims["PP"] = up(W * T // 2, 8)
    dims["N"] = patch_weight.shape[1]
    CB = CH // S
    TILE = R * W
    dims["AM"] = packed_rows(TILE, CB, 16)
    dims["PM"] = packed_rows(2 * TILE, CB, 8)
    dims["WQ"] = 9 * (CB // 4)
    dims["WM"] = packed_rows(dims["WQ"], CB, 8)
    fits = (
        (S, T, C, G) == (4, 2, 2, 2)
        and CH % S == 0
        and CB <= LANES
        and CB % (4 * 8) == 0
        and CB % (CH // NGROUP) == 0
        and TILE % 8 == 0
        and TILE <= LANES
        and R % 2 == 0
        and R <= 8
        and all(dims[name] % 8 == 0 for name in ("AM", "PM", "WQ", "WM"))
        and dims["WM"] > 8
        and 2 * R + 2 <= up(2 * R + 2, 8)
        and head_weight.shape[3] * C == Z
        and Z % 16 == 0
        and 3 * Z <= LANES
        and R * Z <= LANES
        and W * T <= LANES
        and W * T % 2 == 0
        and 4 * Z <= LANES
        and dims["N"] % LANES == 0
    )
    return dims if fits else None


def fused(dims, args):
    S, T, C = dims["S"], dims["T"], dims["C"]
    R, W, CH = dims["R"], dims["W"], dims["CH"]
    Z, FR, N = dims["Z"], dims["FR"], dims["N"]
    CB, NH = CH // S, CH // C
    TILE, REG = R * W, 2 * R * W
    (f, g1, s1, w1, g2, s2, w2, g3, s3, hw, hb, noisy, later, pw, pb) = args
    flat = lambda v: v.reshape((9,) + v.shape[2:])
    by_row = lambda v: jnp.transpose(v, (0, 2, 1, 3))
    operands = (
        f, g1, s1, flat(w1), g2, s2, flat(w2), g3, s3,
        flat(jnp.transpose(hw, (0, 1, 3, 2))), hb, by_row(noisy), by_row(later), pw, pb,
    )
    vmem = pl.BlockSpec(memory_space=pltpu.VMEM)
    far = pl.BlockSpec(memory_space=pl.ANY)
    dma = lambda *shape: pltpu.SemaphoreType.DMA(shape)
    buf = lambda *shape: pltpu.VMEM(shape, F32)
    half = lambda *shape: pltpu.VMEM(shape, BF16)
    PR, PC, PP = dims["PR"], dims["PC"], dims["PP"]
    MR, RR = up(2 * R + 2, 8), up(W + 2, 8)
    TR = up(8 + 2 * W + TILE + LANES, 8)
    scratch = {
        name: pltpu.VMEM(operands[k].shape, F32)
        for name, k in (
            ("feat", 0), ("gain1", 1), ("shift1", 2), ("w1_raw", 3), ("gain2", 4), ("shift2", 5),
            ("w2_raw", 6), ("gain3", 7), ("shift3", 8), ("head_w", 9), ("head_b", 10),
            ("noisy", 11), ("later", 12), ("patch_b", 14),
        )
    }
    scratch |= {
        "pw_raw": buf(N // LANES, pw.shape[0], LANES),
        "prm": buf(3, S, 8, LANES),
        "tile": buf(S, TILE, LANES),
        "feat_all": buf(S, REG, LANES),
        "a_pack": buf(S, dims["AM"], LANES),
        "a_in": buf(2, S, dims["AM"], LANES),
        "st": buf(8, LANES),
        "st_in": buf(T, S, 8, LANES),
        "colf": buf(S, 8, LANES),
        "colf_in": buf(2, S, 8, LANES),
        "rowf": buf(S, RR, LANES),
        "rowf_in": buf(S, RR, LANES),
        "corf": buf(8, LANES),
        "corf_in": buf(8, LANES),
        "wpack": buf(2, 2, C, dims["WM"], LANES),
        "wown": buf(2, 9 * CB, LANES),
        "bias_out": buf(Z // C, LANES),
        "bias_in": buf(Z // C, LANES),
        "wq": buf(2, S, 4, dims["WM"], LANES),
        "wf": buf(9 * CB, LANES),
        "mat": half(2, S, 9 * LANES, 2 * LANES),
        "taps": buf(S, 3, TR, LANES),
        "acc": buf(REG, LANES),
        "conv_raw": buf(S, REG, LANES),
        "ypack": buf(dims["PM"], LANES),
        "yin": buf(3, dims["PM"], LANES),
        "hid": buf(REG, LANES),
        "colm": buf(2, MR, LANES),
        "colm_in": buf(2, MR, LANES),
        "rowm": buf(2, RR, LANES),
        "rowm_in": buf(2, RR, LANES),
        "corm": buf(2, 8, LANES),
        "corm_in": buf(2, 8, LANES),
        "rl_in": buf(S, MR + RR, LANES),
        "hw_send": buf(9, Z // C, LANES),
        "hwq": buf(C, 9, Z // C, LANES),
        "wh_mat": half(LANES, 9 * LANES),
        "wn_mat": half(12 * Z, N),
        "mixed": buf(TR - 8, LANES),
        "lat_send": buf(2, Z, LANES),
        "lat_in": buf(C, S, Z, LANES),
        "cells": buf(LANES, LANES),
        "turned": buf(LANES, LANES),
        "patch": buf(PR * PP, LANES),
        "load_sem": dma(16 + N // LANES),
        "as_sem": dma(3), "ar_sem": dma(2), "fs": dma(2), "fr": dma(2), "gs": dma(2),
        "ss_sem": dma(T, S), "sr_sem": dma(T, S),
        "cs_sem": dma(3), "cr_sem": dma(2),
        "rs_sem": dma(4), "rr_sem": dma(2),
        "os_sem": dma(4), "or_sem": dma(1),
        "is_sem": dma(1), "ir_sem": dma(1),
        "zs": dma(2, S, C), "zr": dma(2, S),
        "ys": dma(2, S), "yr": dma(2, S),
        "bs": dma(2, S, 2), "br": dma(2, S, 2),
        "es": dma(2), "er": dma(2),
        "ks": dma(2, 3), "kr": dma(2, 3),
        "vs": dma(3), "vr": dma(3),
        "ls": dma(3), "lr": dma(S),
        "hs": dma(3), "hr": dma(C),
        "ts": dma(2, T, C), "tr": dma(C, S),
    }
    patch, base, wc, latent = pl.pallas_call(
        functools.partial(fused_kernel, dims, tuple(scratch)),
        out_shape=(
            jax.ShapeDtypeStruct((FR, PR * PP, LANES), F32),
            jax.ShapeDtypeStruct((FR, PR * PP, N), F32),
            jax.ShapeDtypeStruct((12 * Z, N), BF16),
            jax.ShapeDtypeStruct((R, Z, W), F32),
        ),
        in_specs=[pl.BlockSpec(memory_space=pltpu.HBM)] * 15,
        out_specs=(vmem, vmem, vmem, vmem),
        scratch_shapes=list(scratch.values()),
        compiler_params=pltpu.CompilerParams(
            collective_id=0, has_side_effects=True, vmem_limit_bytes=32 * 2**20
        ),
        name="fused_block",
    )(*[pltpu.with_memory_space_constraint(v, pltpu.HBM) for v in operands])
    NB = 4 if N % (4 * LANES) == 0 else 1
    tokens, latent = pl.pallas_call(
        functools.partial(finish_kernel, dims, NB),
        out_shape=(
            jax.ShapeDtypeStruct((PR, PC, FR, N), F32),
            jax.ShapeDtypeStruct((R, Z, W), F32),
        ),
        in_specs=[vmem] * 4,
        out_specs=(pl.BlockSpec(memory_space=pltpu.HBM), pl.BlockSpec(memory_space=pltpu.HBM)),
        scratch_shapes=[buf(PR, PC, FR, N), dma(NB + 1)],
        compiler_params=pltpu.CompilerParams(vmem_limit_bytes=8 * 2**20),
        name="finish_tokens",
    )(patch, base, wc, latent)
    return jnp.transpose(tokens, (2, 0, 1, 3)), jnp.transpose(latent, (0, 2, 1))


def solution(mesh):
    shape = dict(mesh.shape)

    def step(*args):
        dims = plan(shape, args[0], args[11], args[13], args[9])
        return on_device(*args) if dims is None else fused(dims, args)

    return jax.shard_map(
        step,
        mesh=mesh,
        in_specs=(
            P(("groups", "space"), "tm", None),
            P(),
            P(),
            P(None, None, "space", "chan"),
            P(),
            P(),
            P(None, None, "space", "chan"),
            P(),
            P(),
            P(None, None, "space", "chan"),
            P("chan"),
            P(("groups", "tm"), None, "space", None),
            P(("groups", "tm"), None, "space", None),
            P(None, "chan"),
            P("chan"),
        ),
        out_specs=(P(("groups", "tm"), "space", None, "chan"), P(("groups", "space"), "tm", None)),
        check_vma=False,
    )
```

time: 51.9 us -> 47.6 us (0.917)
  Pallas kernels: 51.1 us -> 46.8 us
    pallas_call x2, Pallas kernels: 51.1 us -> 46.8 us  [the longest x1 45.7 us: fused(): pl.pallas_call(functools.partial(fused_kernel, dims, tuple(scratch)), out...]
where the time goes in v1:
time: 47.6 us; the launch traced here: 47.4 us
  Pallas kernels  46.8 us (98%)
  between operations  0.64 us (1%)
    pallas_call x1, Pallas kernels, fused(): pl.pallas_call(functools.partial(fused_kernel, dims, tuple(scratch)), out...  45.7 us
    pallas_call x1, Pallas kernels, fused(): pl.pallas_call(functools.partial(finish_kernel, dims, NB), out_shape=(jax...  1.14 us

profile of v1, /device:TPU:0, one launch (start us, length us, event | category | flops | bytes accessed | tf_op | source)
XLA Modules:
  0.0 47.4 jit_solution(14736628574349577820)
XLA Ops:
  0.6 45.7 %fused_block.1 = (f32[1,72,128]{2,1,0:T(8,128)S(1)}, f32[1,72,2560]{2,1,0:T(8,128)S(1)}, bf16[192,2560]{1,0:T(8,128)(2,1)S(1)}, f32[6,16,20]{2,1,0:T(8,128)S(1)}) custom-call(f32[6,20,384]{2,1,0:T(8,128)} %refs_0_.1, f32[384]{0:T(512)} %refs_1_.1, f32[384]{0:T(512)} %refs_2_.1, f32[9,96,192]{2,1,0:T(8,128)} %bitcast.9, f32[384]{0:T(512)} %refs_4_.1, ...), custom_call_target="tpu_custom_call" | custom-call | tf_op jit(solution)/shard_map/fused_block/pallas_call | solution.py:1008
  46.3 1.1 %finish_tokens.1 = (f32[3,20,1,2560]{3,2,1,0:T(1,128)}, f32[6,16,20]{2,1,0:T(8,128)}) custom-call(f32[1,72,128]{2,1,0:T(8,128)S(1)} %get-tuple-element.8.patch, f32[1,72,2560]{2,1,0:T(8,128)S(1)} %get-tuple-element.9.base, bf16[192,2560]{1,0:T(8,128)(2,1)S(1)} %get-tuple-element.10.wc, f32[6,16,20]{2,1,0:T(8,128)S(1)} %get-tuple-element.11.latent_in), custom_call_target="tpu_custom_call" | custom-call | tf_op jit(solution)/shard_map/finish_tokens/pallas_call | solution.py:1025

commit v2 on v1

--- a/solution.py
+++ b/solution.py
@@ -214,7 +214,6 @@
     near, cross = 2 * t + 1 - p, 2 * tx + 1 - p
     home = c == t
     stray = c != t
-    sent = []
 
     def remote(src, dst, ssem, rsem, **where):
         return pltpu.make_async_remote_copy(
@@ -224,14 +223,17 @@
 
     def go(copy):
         copy.start()
-        sent.append((None, copy))
 
     def go_if(condition, copy):
         @pl.when(condition)
         def _():
             copy.start()
 
-        sent.append((condition, copy))
+    def rows_of(count):
+        return v.wf.at[pl.ds(0, count)]
+
+    def await_bytes(ref, sem):
+        pltpu.make_async_copy(ref, ref, sem).wait()
 
     early = (
         (feat_hbm, v.feat), (w1_hbm, v.w1_raw), (gain1_hbm, v.gain1), (shift1_hbm, v.shift1),
@@ -246,7 +248,7 @@
     strips = v.pw_raw.shape[0]
     loads += [
         pltpu.make_async_copy(
-            pw_hbm.at[:, n * LANES : (n + 1) * LANES], v.pw_raw.at[n], v.load_sem.at[len(early) + n]
+            pw_hbm.at[:, n * LANES : (n + 1) * LANES], v.pw_raw.at[n], v.load_sem.at[len(early)]
         )
         for n in range(strips)
     ]
@@ -362,7 +364,7 @@
         v.mat[k, q, tap * LANES : tap * LANES + CB, LANES : 2 * LANES] = low
 
     def own_copy(k):
-        return remote(v.wown.at[k], v.wown.at[k], v.es.at[k], v.er.at[k], chan=oc)
+        return remote(v.wown.at[k], v.wown.at[k], v.es.at[0], v.er.at[k], chan=oc)
 
     def own_mat(k):
         pl.when(stray)(own_copy(k).wait_recv)
@@ -375,41 +377,48 @@
             for tap in range(9):
                 v.mat[k, q, tap * LANES + CB : (tap + 1) * LANES, :] = gap
 
-    def z_copy(k, peer, slot, cc):
+    def z_copy(k, n, peer, slot, cc):
         return remote(
             v.wpack.at[k, lax.rem(peer, 2), cc], v.wq.at[k, slot, 2 * g + cc],
-            v.zs.at[k, peer, cc], v.zr.at[k, slot], space=peer, chan=cc,
-        )
-
-    def y_copy(k, z, which):
+            v.zs.at[0], v.zr.at[k, n], space=peer, chan=cc,
+        )
+
+    def y_copy(k, n, z, which):
         ref = v.wq.at[k, z, which]
-        return remote(ref, ref, v.ys.at[k, z], v.yr.at[k, z], groups=gy)
-
-    def b_copy(k, z, which, n):
+        return remote(ref, ref, v.ys.at[0], v.yr.at[k, n], groups=gy)
+
+    def b_copy(k, n, z, which):
         ref = v.wq.at[k, z, which]
-        return remote(ref, ref, v.bs.at[k, z, n], v.br.at[k, z, n], chan=oc)
+        return remote(ref, ref, v.bs.at[0], v.br.at[k, n], chan=oc)
 
     order = (far, far2, pair)
 
-    def z_send(k, z):
+    def z_send(k, n):
         for cc in range(C):
-            go_if(home, z_copy(k, z, s, cc))
-
-    def relay(k, z):
+            go_if(home, z_copy(k, n, order[n], s, cc))
+
+    def relay(k, n):
+        z = order[n]
         remote(
-            v.wpack.at[k, 0, 0], v.wq.at[k, z, 2 * g + c], v.zs.at[k, z, 0], v.zr.at[k, z],
+            v.wpack.at[k, 0, 0], v.wq.at[k, z, 2 * g + c], v.zs.at[0], v.zr.at[k, n],
             space=z, chan=t,
         ).wait_recv()
-        go(y_copy(k, z, 2 * g + c))
-        go(b_copy(k, z, 2 * g + c, 0))
-
-    def relay2(k, z):
-        y_copy(k, z, 2 * gy + c).wait_recv()
-        go(b_copy(k, z, 2 * gy + c, 1))
-
-    def finish_weights(k, z):
-        b_copy(k, z, 2 * g + oc, 0).wait_recv()
-        b_copy(k, z, 2 * gy + oc, 1).wait_recv()
+        y_copy(k, n, z, 2 * g + c).start()
+        b_copy(k, n, z, 2 * g + c).start()
+
+    def relay2(k, n, z):
+        y_copy(k, n, z, 2 * gy + c).wait_recv()
+        b_copy(k, n, z, 2 * gy + c).start()
+
+    def nth_weights(i):
+        flip = lax.rem(lax.div(i + 1, 2), 2)
+        return 2 * lax.rem(hh + flip, 2) + lax.rem(p + lax.div(i, 2), 2)
+
+    def nth_block(j):
+        return 2 * lax.rem(t + lax.rem(j, 2), 2) + lax.rem(p + lax.div(j, 2), 2)
+
+    def finish_weights(k, n, z):
+        await_bytes(rows_of(2 * WM), v.br.at[k, n])
         for kk in range(4):
             at = 0
             for value in unpack(v.wq[k, z, kk], WQ):
@@ -423,32 +432,31 @@
 
     pl.semaphore_wait(barrier, S * T * C)
 
-    def feat_copy(n, slot, **where):
-        return remote(v.a_pack, v.a_in.at[slot], v.as_sem.at[n], v.ar_sem.at[slot], **where)
+    feat_copy = remote(v.a_pack, v.a_in.at[p], v.as_sem.at[0], v.ar_sem.at[0], tm=tx)
 
     def feat_part(m):
         blocks = pl.ds(2 * m, 2)
         return remote(
-            v.a_pack.at[blocks], v.a_in.at[p, blocks], v.fs.at[m], v.fr.at[m], space=pair
+            v.a_pack.at[blocks], v.a_in.at[p, blocks], v.fs.at[0], v.fr.at[m], space=pair
         )
 
     def st_copy(dt, peer, mt, ms):
         return remote(
-            v.st, v.st_in.at[mt, ms], v.ss_sem.at[dt, peer], v.sr_sem.at[mt, ms],
+            v.st, v.st_in.at[mt, ms], v.ss_sem.at[0], v.sr_sem.at[0],
             space=peer, tm=tx if dt else t,
         )
 
     def col_copy(n, slot, **where):
-        return remote(v.colf, v.colf_in.at[slot], v.cs_sem.at[n], v.cr_sem.at[slot], **where)
+        return remote(v.colf, v.colf_in.at[slot], v.cs_sem.at[0], v.cr_sem.at[slot], **where)
 
     hub = inner & home
     row_copy = remote(v.rowf, v.rowf_in, v.rs_sem.at[0], v.rr_sem.at[0], space=far2)
 
     def row_forward(n, **where):
-        return remote(v.rowf_in, v.rowf_in, v.rs_sem.at[1 + n], v.rr_sem.at[1], **where)
+        return remote(v.rowf_in, v.rowf_in, v.rs_sem.at[1], v.rr_sem.at[1], **where)
 
     def cor_copy(n, **where):
-        return remote(v.corf, v.corf_in, v.os_sem.at[n], v.or_sem.at[0], **where)
+        return remote(v.corf, v.corf_in, v.os_sem.at[0], v.or_sem.at[0], **where)
 
     st_peers = [(0, far), (0, far2), (1, far), (1, far2), (0, pair), (1, pair), (1, s)]
     go_if(hub, row_copy)
@@ -461,14 +469,15 @@
     go_if(stray, col_copy(2, p, space=pair, tm=tx))
     go_if(home, feat_part(0))
     go_if(home, feat_part(1))
-    go_if(home, feat_copy(0, p, tm=tx))
-    z_send(0, far)
+    go_if(home, feat_copy)
+    z_send(0, 0)
     go_if(home, own_copy(0))
-    z_send(0, far2)
+    z_send(0, 1)
     bias_copy = remote(v.bias_out, v.bias_in, v.is_sem.at[0], v.ir_sem.at[0], chan=oc)
 
-    for load in loads[2:]:
+    for load in loads[2 : len(early)]:
         load.wait()
+    await_bytes(v.pw_raw, v.load_sem.at[len(early)])
     for n, (gain, shift) in enumerate(
         ((v.gain1, v.shift1), (v.gain2, v.shift2), (v.gain3, v.shift3))
     ):
@@ -493,21 +502,30 @@
 
     for n, where in enumerate((dict(space=pair), dict(tm=tx), dict(space=pair, tm=tx))):
         go_if(hub, row_forward(n, **where))
-    z_send(0, pair)
+    z_send(0, 2)
     w_pack(1, v.w2_raw)
     w_own(1, v.w2_raw)
     go_if(home, own_copy(1))
     def feat_pass(m):
         ref = v.a_in.at[1 - p, pl.ds(2 * m, 2)]
-        return remote(ref, ref, v.gs.at[m], v.fr.at[m], tm=tx)
-
-    relay(0, far)
-    for m in range(2):
-        pl.when(home)(feat_part(m).wait_recv)
-        go_if(home, feat_pass(m))
+        return remote(ref, ref, v.gs.at[0], v.fr.at[m], tm=tx)
+
+    def pass_features(when):
+        @pl.when(home & when)
+        def _():
+            for m in range(2):
+                feat_part(m).wait_recv()
+                feat_pass(m).start()
+
+    pass_features(inner)
+    relay(0, 0)
+    pass_features(jnp.logical_not(inner))
+    for n in (0, 2, 1):
+        z_send(1, n)
+    relay(0, 1)
 
     def hw_copy(n, slot, **where):
-        return remote(v.hw_send, v.hwq.at[slot], v.hs.at[n], v.hr.at[slot], **where)
+        return remote(v.hw_send, v.hwq.at[slot], v.hs.at[0], v.hr.at[slot], **where)
 
     @pl.when(hh == t)
     def _():
@@ -523,7 +541,7 @@
 
     @pl.when(stray)
     def _():
-        feat_copy(0, p, tm=tx).wait_recv()
+        feat_copy.wait_recv()
         unpack_features(p)
 
     @pl.when(stray)
@@ -532,15 +550,12 @@
             feat_pass(m).wait_recv()
 
     unpack_features(1 - p)
-    for dt, peer in st_peers:
-        st_copy(dt, peer, tx if dt else t, peer).wait_recv()
+    await_bytes(rows_of(8 * len(st_peers)), v.sr_sem.at[0])
     col_copy(1, 1 - p, space=pair).wait_recv()
     pl.when(home)(col_copy(0, p, tm=tx).wait_recv)
     cor_copy(0, space=far).wait_recv()
     pl.when(jnp.logical_not(hub))(row_forward(0, space=pair).wait_recv)
 
-    for z in order:
-        z_send(1, z)
     scale = 1.0 / float(per_group * TILE * S * T)
     everyone = [v.st_in[tt, ss] for tt in range(T) for ss in range(S)]
     total8 = everyone[0]
@@ -585,13 +600,18 @@
                 v.taps[q, 0, pl.ds(at, count, stride=W), :] = from_left
                 v.taps[q, 2, pl.ds(at + W - 1, count, stride=W), :] = from_right
 
-    def first_taps(q):
+    for q in range(S):
+        v.nrm[q, 0:1, :] = center8[q : q + 1]
+        v.nrm[q, 1:2, :] = inverse4[q : q + 1]
+        v.nrm[q, 2:3, :] = v.corf_in[q : q + 1, :]
+
+    def first_taps(q, carry):
         build_taps(
             0, q, v.feat_all[q],
             [(0, R, v.colf_in[0, q, 0:R, :]), (R, R, v.colf_in[1, q, 0:R, :])],
-            v.corf_in[q : q + 1, :], v.rowf_in[q, 0:W, :],
-            center8[q : q + 1], inverse4[q : q + 1],
-        )
+            v.nrm[q, 2:3, :], v.rowf_in[q, 0:W, :], v.nrm[q, 0:1, :], v.nrm[q, 1:2, :],
+        )
+        return carry
 
     def operand(q):
         highs, lows = [], []
@@ -608,25 +628,31 @@
         part = jnp.dot(operand(q), v.mat[k, q], preferred_element_type=F32)
         return part[0:REG, 0:LANES] + part[0:REG, LANES:] + part[REG:, 0:LANES]
 
-    for q in range(S):
-        first_taps(q)
-    relay(0, far2)
-    relay2(0, far)
-    v.acc[...] = conv_block(0, s)
-    relay(0, pair)
+    lax.fori_loop(0, S, first_taps, 0)
+    relay2(0, 0, far)
+    relay(0, 2)
     go_if(hh == t, hw_copy(0, c, chan=oc))
     go_if(hh == t, hw_copy(1, c, space=far))
     go_if(hh == t, hw_copy(2, c, space=far, chan=oc))
-    relay2(0, far2)
-    finish_weights(0, far)
-    v.acc[...] += conv_block(0, far)
-    relay(1, far)
-    relay2(0, pair)
-    finish_weights(0, far2)
-    v.acc[...] += conv_block(0, far2)
-    own_mat(1)
-    finish_weights(0, pair)
-    first = v.acc[...] + conv_block(0, pair)
+    v.acc[...] = jnp.zeros(v.acc.shape, F32)
+
+    def first_step(i, carry):
+        z = nth_weights(i)
+
+        @pl.when(i > 0)
+        def _():
+            finish_weights(0, i - 1, z)
+
+        v.acc[...] += conv_block(0, z)
+
+        @pl.when(i < 2)
+        def _():
+            relay2(0, i + 1, nth_weights(i + 2))
+
+        return carry
+
+    lax.fori_loop(0, 4, first_step, 0)
+    first = v.acc[...]
     v.conv_raw[own] = first
 
     def rim_exchange(k, full):
@@ -642,17 +668,16 @@
             ref[k, first : first + 1, :] = total
             ref[k, first + 1 : first + 2, :] = spread
         copies = [
-            remote(v.corm.at[k], v.corm_in.at[k], v.ks.at[k, 0], v.kr.at[k, 0], space=far, chan=oc),
-            remote(v.rowm.at[k], v.rowm_in.at[k], v.ks.at[k, 1], v.kr.at[k, 1], space=far),
-            remote(v.colm.at[k], v.colm_in.at[k], v.ks.at[k, 2], v.kr.at[k, 2], chan=oc),
+            remote(v.corm.at[k], v.corm_in.at[k], v.ks.at[0], v.kr.at[k], space=far, chan=oc),
+            remote(v.rowm.at[k], v.rowm_in.at[k], v.ks.at[0], v.kr.at[k], space=far),
+            remote(v.colm.at[k], v.colm_in.at[k], v.ks.at[0], v.kr.at[k], chan=oc),
         ]
         for copy in copies:
             go(copy)
-        return copies, total, spread
-
-    def rim_finish(k, copies, total, spread):
-        for copy in copies:
-            copy.wait_recv()
+        return total, spread
+
+    def rim_finish(k, total, spread):
+        await_bytes(rows_of(MR + up(W + 2, 8) + 8), v.kr.at[k])
         parts = [(total, spread)]
         for ref, first in ((v.rowm_in, W), (v.colm_in, 2 * R), (v.corm_in, 1)):
             parts.append((ref[k, first : first + 1, :], ref[k, first + 1 : first + 2, :]))
@@ -670,12 +695,13 @@
     pack(v.ypack, first, PM)
     near_copy = remote(v.ypack, v.yin.at[0], v.vs.at[0], v.vr.at[0], space=pair)
     go(near_copy)
-    side_copy = remote(v.ypack, v.yin.at[2], v.vs.at[1], v.vr.at[1], tm=tx)
+    side_copy = remote(v.ypack, v.yin.at[2], v.vs.at[0], v.vr.at[1], tm=tx)
     go(side_copy)
-    cross_copy = remote(v.yin.at[0], v.yin.at[1], v.vs.at[2], v.vr.at[2], tm=tx)
-    relay(1, far2)
-    relay(1, pair)
-    relay2(1, far)
+    cross_copy = remote(v.yin.at[0], v.yin.at[1], v.vs.at[0], v.vr.at[2], tm=tx)
+    own_mat(1)
+    relay(1, 0)
+    relay(1, 2)
+    relay(1, 1)
     center, inverse = rim_finish(0, *rims1)
     v.rl_in[own, 0 : 2 * R, :] = v.colm_in[0, 0 : 2 * R, :]
     v.rl_in[own, 2 * R : 2 * R + 1, :] = v.corm_in[0, 0:1, :]
@@ -685,7 +711,7 @@
 
     def rl_copy(n, q, **where):
         ref = v.rl_in.at[q]
-        return remote(ref, ref, v.ls.at[n], v.lr.at[q], **where)
+        return remote(ref, ref, v.ls.at[0], v.lr.at[q], **where)
 
     go(rl_copy(0, own, space=pair))
     go(rl_copy(1, own, space=pair, tm=tx))
@@ -698,36 +724,55 @@
             v.rl_in[q, 2 * R + 1 : 2 * R + 2, :], v.rl_in[q, 2 * R + 2 : 2 * R + 3, :],
         )
 
-    second_taps(own)
-    relay2(1, far2)
-    near_copy.wait_recv()
-    go(cross_copy)
-    finish_weights(1, far)
-    v.acc[...] = conv_block(1, own)
-
-    def unpack_conv(slot, q):
-        at = 0
-        for value in unpack(v.yin[slot], REG):
-            v.conv_raw[q, at : at + value.shape[0], :] = value
-            at += value.shape[0]
-
-    side_copy.wait_recv()
-    rl_copy(2, side, tm=tx).wait_recv()
-    unpack_conv(2, side)
-    second_taps(side)
-    relay2(1, pair)
-    v.acc[...] += conv_block(1, side)
-    rl_copy(0, near, space=pair).wait_recv()
-    unpack_conv(0, near)
-    second_taps(near)
-    cross_copy.wait_recv()
-    rl_copy(1, cross, space=pair, tm=tx).wait_recv()
-    unpack_conv(1, cross)
-    second_taps(cross)
-    finish_weights(1, far2)
-    v.acc[...] += conv_block(1, far2)
-    finish_weights(1, pair)
-    v.hid[...] = v.acc[...] + conv_block(1, pair) + v.feat_all[own]
+    def second_step(j, carry):
+        q = nth_block(j)
+
+        @pl.when(j == 1)
+        def _():
+            side_copy.wait_recv()
+            rl_copy(2, side, tm=tx).wait_recv()
+
+        @pl.when(j == 2)
+        def _():
+            rl_copy(0, near, space=pair).wait_recv()
+
+        @pl.when(j == 3)
+        def _():
+            cross_copy.wait_recv()
+            rl_copy(1, cross, space=pair, tm=tx).wait_recv()
+
+        @pl.when(j > 0)
+        def _():
+            at = 0
+            for value in unpack(v.yin[lax.rem(j + 1, 3)], REG):
+                v.conv_raw[q, at : at + value.shape[0], :] = value
+                at += value.shape[0]
+
+        second_taps(q)
+
+        @pl.when(j == 0)
+        def _():
+            relay2(1, 0, far)
+            near_copy.wait_recv()
+            cross_copy.start()
+            relay2(1, 2, pair)
+            finish_weights(1, 0, far)
+
+        @pl.when(j == 1)
+        def _():
+            relay2(1, 1, far2)
+
+        @pl.when(j == 2)
+        def _():
+            finish_weights(1, 2, pair)
+            finish_weights(1, 1, far2)
+
+        v.acc[...] += conv_block(1, q)
+        return carry
+
+    v.acc[...] = v.feat_all[own]
+    lax.fori_loop(0, S, second_step, 0)
+    v.hid[...] = v.acc[...]
     rims2 = rim_exchange(1, v.hid)
 
     @pl.when(hh == t)
@@ -823,7 +868,7 @@
     def lat_copy(dp, dt, dc, slot_c, slot_q):
         return remote(
             v.lat_send.at[1 - p if dp else p], v.lat_in.at[slot_c, slot_q],
-            v.ts.at[dp, dt, dc], v.tr.at[slot_c, slot_q],
+            v.ts.at[0], v.tr.at[0],
             space=pair if dp else s, tm=tx if dt else t, chan=oc if dc else c,
         )
 
@@ -831,16 +876,9 @@
     for dp, dt, dc in hops:
         go_if(((tx if dt else t) == 0) | (c == 1), lat_copy(dp, dt, dc, c, own))
 
-    for condition, copy in sent:
-        if condition is None:
-            copy.wait_send()
-        else:
-            pl.when(condition)(copy.wait_send)
-
-    for dp, dt, dc in hops:
-        from_c = oc if dc else c
-        source = 2 * (tx if dt else t) + (1 - p if dp else p)
-        pl.when((t == 0) | (from_c == 1))(lat_copy(dp, dt, dc, from_c, source).wait_recv)
+    pl.when(t == 0)(functools.partial(await_bytes, rows_of(7 * Z), v.tr.at[0]))
+    pl.when((t == 1) & (c == 1))(functools.partial(await_bytes, rows_of(3 * Z), v.tr.at[0]))
+    pl.when((t == 1) & (c == 0))(functools.partial(await_bytes, rows_of(4 * Z), v.tr.at[0]))
 
     def latent_of(tt):
         return v.lat_in[tt, 0] + v.lat_in[tt, 1] + v.lat_in[tt, 2] + v.lat_in[tt, 3]
@@ -860,6 +898,23 @@
             cells[rows, 0:FULLW] = jnp.where(opening, cells[rows, 0:FULLW], v.later[f, i])
         build_patches()
         patch_out[f] = patch[...]
+    RR = up(W + 2, 8)
+    drains = (
+        (home, rows_of(S * AM), v.as_sem), (home, rows_of(S * AM), v.fs),
+        (home, rows_of(S * AM), v.gs), (None, rows_of(8 * len(st_peers)), v.ss_sem),
+        (stray, rows_of(3 * S * 8), v.cs_sem), (hub, rows_of(S * RR), v.rs_sem),
+        (inner & stray, rows_of(4 * 8), v.os_sem), (None, rows_of(ZH), v.is_sem),
+        (home, v.wq.at[0, pl.ds(0, 3)], v.zs), (None, v.wq.at[0, pl.ds(0, 3), pl.ds(0, 2)], v.ys),
+        (None, v.wq.at[0, pl.ds(0, 3)], v.bs), (home, v.wown, v.es),
+        (None, rows_of(2 * (MR + RR + 8)), v.ks), (None, v.yin, v.vs),
+        (None, rows_of(3 * (MR + RR)), v.ls), (hh == t, rows_of(3 * 9 * ZH), v.hs),
+        (c == 1, rows_of(7 * Z), v.ts), ((c == 0) & (t == 0), rows_of(3 * Z), v.ts),
+        ((c == 0) & (t == 1), rows_of(4 * Z), v.ts),
+    )
+    for condition, ref, sem in drains:
+        wait = functools.partial(await_bytes, ref, sem.at[0])
+        wait() if condition is None else pl.when(condition)(wait)
+    pl.when(hub)(functools.partial(await_bytes, rows_of(3 * S * RR), v.rs_sem.at[1]))
 
 
 def up(value, unit):
@@ -966,6 +1021,7 @@
         "wf": buf(9 * CB, LANES),
         "mat": half(2, S, 9 * LANES, 2 * LANES),
         "taps": buf(S, 3, TR, LANES),
+        "nrm": buf(S, 8, LANES),
         "acc": buf(REG, LANES),
         "conv_raw": buf(S, REG, LANES),
         "ypack": buf(dims["PM"], LANES),
@@ -988,22 +1044,22 @@
         "cells": buf(LANES, LANES),
         "turned": buf(LANES, LANES),
         "patch": buf(PR * PP, LANES),
-        "load_sem": dma(16 + N // LANES),
-        "as_sem": dma(3), "ar_sem": dma(2), "fs": dma(2), "fr": dma(2), "gs": dma(2),
-        "ss_sem": dma(T, S), "sr_sem": dma(T, S),
-        "cs_sem": dma(3), "cr_sem": dma(2),
-        "rs_sem": dma(4), "rr_sem": dma(2),
-        "os_sem": dma(4), "or_sem": dma(1),
+        "load_sem": dma(15),
+        "as_sem": dma(1), "ar_sem": dma(1), "fs": dma(1), "fr": dma(2), "gs": dma(1),
+        "ss_sem": dma(1), "sr_sem": dma(1),
+        "cs_sem": dma(1), "cr_sem": dma(2),
+        "rs_sem": dma(2), "rr_sem": dma(2),
+        "os_sem": dma(1), "or_sem": dma(1),
         "is_sem": dma(1), "ir_sem": dma(1),
-        "zs": dma(2, S, C), "zr": dma(2, S),
-        "ys": dma(2, S), "yr": dma(2, S),
-        "bs": dma(2, S, 2), "br": dma(2, S, 2),
-        "es": dma(2), "er": dma(2),
-        "ks": dma(2, 3), "kr": dma(2, 3),
-        "vs": dma(3), "vr": dma(3),
-        "ls": dma(3), "lr": dma(S),
-        "hs": dma(3), "hr": dma(C),
-        "ts": dma(2, T, C), "tr": dma(C, S),
+        "zs": dma(1), "zr": dma(2, 3),
+        "ys": dma(1), "yr": dma(2, 3),
+        "bs": dma(1), "br": dma(2, 3),
+        "es": dma(1), "er": dma(2),
+        "ks": dma(1), "kr": dma(2),
+        "vs": dma(1), "vr": dma(3),
+        "ls": dma(1), "lr": dma(S),
+        "hs": dma(1), "hr": dma(C),
+        "ts": dma(1), "tr": dma(1),
     }
     patch, base, wc, latent = pl.pallas_call(
         functools.partial(fused_kernel, dims, tuple(scratch)),

time: 47.6 us -> 44.4 us (0.933)
  Pallas kernels: 46.8 us -> 43.6 us
    pallas_call x1, Pallas kernels: 45.7 us -> 42.5 us  [fused(): pl.pallas_call(functools.partial(fused_kernel, dims, tuple(scratch)), out...]
where the time goes in v2:
time: 44.4 us; the launch traced here: 44.2 us
  Pallas kernels  43.6 us (98%)
  between operations  0.64 us (1%)
    pallas_call x1, Pallas kernels, fused(): pl.pallas_call(functools.partial(fused_kernel, dims, tuple(scratch)), out...  42.5 us
    pallas_call x1, Pallas kernels, fused(): pl.pallas_call(functools.partial(finish_kernel, dims, NB), out_shape=(jax...  1.12 us

profile of v2, /device:TPU:0, one launch (start us, length us, event | category | flops | bytes accessed | tf_op | source)
XLA Modules:
  0.0 44.2 jit_solution(1984918396490992349)
XLA Ops:
  0.6 42.5 %fused_block.1 = (f32[1,72,128]{2,1,0:T(8,128)S(1)}, f32[1,72,2560]{2,1,0:T(8,128)S(1)}, bf16[192,2560]{1,0:T(8,128)(2,1)S(1)}, f32[6,16,20]{2,1,0:T(8,128)S(1)}) custom-call(f32[6,20,384]{2,1,0:T(8,128)} %refs_0_.1, f32[384]{0:T(512)} %refs_1_.1, f32[384]{0:T(512)} %refs_2_.1, f32[9,96,192]{2,1,0:T(8,128)} %bitcast.9, f32[384]{0:T(512)} %refs_4_.1, ...), custom_call_target="tpu_custom_call" | custom-call | tf_op jit(solution)/shard_map/fused_block/pallas_call | solution.py:1064
  43.1 1.1 %finish_tokens.1 = (f32[3,20,1,2560]{3,2,1,0:T(1,128)}, f32[6,16,20]{2,1,0:T(8,128)}) custom-call(f32[1,72,128]{2,1,0:T(8,128)S(1)} %get-tuple-element.8.patch, f32[1,72,2560]{2,1,0:T(8,128)S(1)} %get-tuple-element.9.base, bf16[192,2560]{1,0:T(8,128)(2,1)S(1)} %get-tuple-element.10.wc, f32[6,16,20]{2,1,0:T(8,128)S(1)} %get-tuple-element.11.latent_in), custom_call_target="tpu_custom_call" | custom-call | tf_op jit(solution)/shard_map/finish_tokens/pallas_call | solution.py:1081

commit v3 on v2

--- a/solution.py
+++ b/solution.py
@@ -235,26 +235,6 @@
     def await_bytes(ref, sem):
         pltpu.make_async_copy(ref, ref, sem).wait()
 
-    early = (
-        (feat_hbm, v.feat), (w1_hbm, v.w1_raw), (gain1_hbm, v.gain1), (shift1_hbm, v.shift1),
-        (w2_hbm, v.w2_raw), (gain2_hbm, v.gain2), (shift2_hbm, v.shift2),
-        (gain3_hbm, v.gain3), (shift3_hbm, v.shift3), (head_w_hbm, v.head_w),
-        (head_b_hbm, v.head_b), (noisy_hbm, v.noisy), (later_hbm, v.later),
-        (patch_b_hbm, v.patch_b),
-    )
-    loads = [
-        pltpu.make_async_copy(src, dst, v.load_sem.at[k]) for k, (src, dst) in enumerate(early)
-    ]
-    strips = v.pw_raw.shape[0]
-    loads += [
-        pltpu.make_async_copy(
-            pw_hbm.at[:, n * LANES : (n + 1) * LANES], v.pw_raw.at[n], v.load_sem.at[len(early)]
-        )
-        for n in range(strips)
-    ]
-    for load in loads:
-        load.start()
-
     v.lat_in[...] = jnp.zeros(v.lat_in.shape, F32)
     barrier = pltpu.get_barrier_semaphore()
     for ds in range(S):
@@ -273,6 +253,26 @@
                     )
     pl.semaphore_signal(barrier, inc=1, device_id={"groups": gy}, device_id_type=MESH)
 
+    early = (
+        (feat_hbm, v.feat), (w1_hbm, v.w1_raw), (gain1_hbm, v.gain1), (shift1_hbm, v.shift1),
+        (w2_hbm, v.w2_raw), (gain2_hbm, v.gain2), (shift2_hbm, v.shift2),
+        (gain3_hbm, v.gain3), (shift3_hbm, v.shift3), (head_w_hbm, v.head_w),
+        (head_b_hbm, v.head_b), (noisy_hbm, v.noisy), (later_hbm, v.later),
+        (patch_b_hbm, v.patch_b),
+    )
+    loads = [
+        pltpu.make_async_copy(src, dst, v.load_sem.at[k]) for k, (src, dst) in enumerate(early)
+    ]
+    strips = v.pw_raw.shape[0]
+    loads += [
+        pltpu.make_async_copy(
+            pw_hbm.at[:, n * LANES : (n + 1) * LANES], v.pw_raw.at[n], v.load_sem.at[len(early)]
+        )
+        for n in range(strips)
+    ]
+    for load in loads:
+        load.start()
+
     def padded(values, width=LANES):
         rows = values.shape[0]
         if width == values.shape[1]:
@@ -348,7 +348,6 @@
                     jnp.where(p == 0, w[:, 0:CB], w[:, CB : 2 * CB])
                 )
 
-    w_own(0, v.w1_raw)
 
     row_id = lax.broadcasted_iota(jnp.int32, (LANES, LANES), 0)
     col_id = lax.broadcasted_iota(jnp.int32, (LANES, LANES), 1)
@@ -471,8 +470,9 @@
     go_if(home, feat_part(1))
     go_if(home, feat_copy)
     z_send(0, 0)
+    z_send(0, 1)
+    w_own(0, v.w1_raw)
     go_if(home, own_copy(0))
-    z_send(0, 1)
     bias_copy = remote(v.bias_out, v.bias_in, v.is_sem.at[0], v.ir_sem.at[0], chan=oc)
 
     for load in loads[2 : len(early)]:
@@ -492,7 +492,6 @@
     my_bias = jnp.sum(jnp.where(diagonal, bias_row, 0.0), axis=1, keepdims=True)
     v.bias_out[...] = jnp.broadcast_to(my_bias, (ZH, LANES))
     go(bias_copy)
-    own_mat(0)
     for tap in range(9):
         v.hw_send[tap] = padded(v.head_w[tap])
 
@@ -503,6 +502,7 @@
     for n, where in enumerate((dict(space=pair), dict(tm=tx), dict(space=pair, tm=tx))):
         go_if(hub, row_forward(n, **where))
     z_send(0, 2)
+    own_mat(0)
     w_pack(1, v.w2_raw)
     w_own(1, v.w2_raw)
     go_if(home, own_copy(1))
@@ -631,9 +631,6 @@
     lax.fori_loop(0, S, first_taps, 0)
     relay2(0, 0, far)
     relay(0, 2)
-    go_if(hh == t, hw_copy(0, c, chan=oc))
-    go_if(hh == t, hw_copy(1, c, space=far))
-    go_if(hh == t, hw_copy(2, c, space=far, chan=oc))
     v.acc[...] = jnp.zeros(v.acc.shape, F32)
 
     def first_step(i, carry):
@@ -648,6 +645,10 @@
         @pl.when(i < 2)
         def _():
             relay2(0, i + 1, nth_weights(i + 2))
+
+        @pl.when(i == 2)
+        def _():
+            relay(1, 0)
 
         return carry
 
@@ -697,9 +698,15 @@
     go(near_copy)
     side_copy = remote(v.ypack, v.yin.at[2], v.vs.at[0], v.vr.at[1], tm=tx)
     go(side_copy)
-    cross_copy = remote(v.yin.at[0], v.yin.at[1], v.vs.at[0], v.vr.at[2], tm=tx)
+    PH = up(PM // 2, 8)
+    upper, lower = pl.ds(0, PH), pl.ds(PH, PM - PH)
+    cross_x = remote(
+        v.yin.at[0, upper], v.yin.at[1, upper], v.vs.at[0], v.vr.at[2], tm=tx
+    )
+    cross_z = remote(
+        v.yin.at[2, lower], v.yin.at[1, lower], v.vs.at[0], v.vr.at[2], space=pair
+    )
     own_mat(1)
-    relay(1, 0)
     relay(1, 2)
     relay(1, 1)
     center, inverse = rim_finish(0, *rims1)
@@ -716,6 +723,8 @@
     go(rl_copy(0, own, space=pair))
     go(rl_copy(1, own, space=pair, tm=tx))
     go(rl_copy(2, own, tm=tx))
+    go_if(hh == t, hw_copy(0, c, chan=oc))
+    go_if(hh == t, hw_copy(1, c, space=far))
 
     def second_taps(q):
         build_taps(
@@ -729,17 +738,26 @@
 
         @pl.when(j == 1)
         def _():
-            side_copy.wait_recv()
+            relay2(1, 2, pair)
             rl_copy(2, side, tm=tx).wait_recv()
 
         @pl.when(j == 2)
         def _():
+            relay2(1, 1, far2)
+
+        @pl.when(j == 2)
+        def _():
             rl_copy(0, near, space=pair).wait_recv()
 
         @pl.when(j == 3)
         def _():
-            cross_copy.wait_recv()
+            await_bytes(rows_of(PM), v.vr.at[2])
             rl_copy(1, cross, space=pair, tm=tx).wait_recv()
+
+        @pl.when((j == 3) & (hh != t))
+        def _():
+            hw_copy(1, c, space=far).wait_recv()
+            remote(v.hwq.at[c], v.hwq.at[c], v.hs.at[0], v.hr.at[c], chan=oc).start()
 
         @pl.when(j > 0)
         def _():
@@ -753,21 +771,28 @@
         @pl.when(j == 0)
         def _():
             relay2(1, 0, far)
+
+        @pl.when(j == jnp.where(t == hh, 1, 0))
+        def _():
+            finish_weights(1, 0, far)
+
+        @pl.when(j == 2)
+        def _():
+            finish_weights(1, 2 - lax.rem(t + hh, 2), near)
+
+        @pl.when(j == 3)
+        def _():
+            finish_weights(1, 1 + lax.rem(t + hh, 2), cross)
+
+        v.acc[...] += conv_block(1, q)
+
+        @pl.when(j == 0)
+        def _():
+            side_copy.wait_recv()
+            cross_z.start()
             near_copy.wait_recv()
-            cross_copy.start()
-            relay2(1, 2, pair)
-            finish_weights(1, 0, far)
-
-        @pl.when(j == 1)
-        def _():
-            relay2(1, 1, far2)
-
-        @pl.when(j == 2)
-        def _():
-            finish_weights(1, 2, pair)
-            finish_weights(1, 1, far2)
-
-        v.acc[...] += conv_block(1, q)
+            cross_x.start()
+
         return carry
 
     v.acc[...] = v.feat_all[own]
@@ -775,15 +800,7 @@
     v.hid[...] = v.acc[...]
     rims2 = rim_exchange(1, v.hid)
 
-    @pl.when(hh == t)
-    def _():
-        hw_copy(0, oc, chan=oc).wait_recv()
-
-    @pl.when(hh != t)
-    def _():
-        for slot in range(C):
-            hw_copy(1, slot, space=far).wait_recv()
-
+    hw_copy(0, oc, chan=oc).wait_recv()
     bias_copy.wait_recv()
     blank = jnp.zeros((LANES - 3 * Z, LANES), F32)
     for b in range(3):
@@ -907,7 +924,8 @@
         (home, v.wq.at[0, pl.ds(0, 3)], v.zs), (None, v.wq.at[0, pl.ds(0, 3), pl.ds(0, 2)], v.ys),
         (None, v.wq.at[0, pl.ds(0, 3)], v.bs), (home, v.wown, v.es),
         (None, rows_of(2 * (MR + RR + 8)), v.ks), (None, v.yin, v.vs),
-        (None, rows_of(3 * (MR + RR)), v.ls), (hh == t, rows_of(3 * 9 * ZH), v.hs),
+        (None, rows_of(3 * (MR + RR)), v.ls), (hh == t, rows_of(2 * 9 * ZH), v.hs),
+        (hh != t, rows_of(9 * ZH), v.hs),
         (c == 1, rows_of(7 * Z), v.ts), ((c == 0) & (t == 0), rows_of(3 * Z), v.ts),
         ((c == 0) & (t == 1), rows_of(4 * Z), v.ts),
     )

time: 44.4 us -> 43.2 us (0.973)
  Pallas kernels: 43.6 us -> 42.4 us
    pallas_call x1, Pallas kernels: 42.5 us -> 41.3 us  [fused(): pl.pallas_call(functools.partial(fused_kernel, dims, tuple(scratch)), out...]
where the time goes in v3:
time: 43.2 us; the launch traced here: 43.1 us
  Pallas kernels  42.4 us (98%)
  between operations  0.64 us (1%)
    pallas_call x1, Pallas kernels, fused(): pl.pallas_call(functools.partial(fused_kernel, dims, tuple(scratch)), out...  41.3 us
    pallas_call x1, Pallas kernels, fused(): pl.pallas_call(functools.partial(finish_kernel, dims, NB), out_shape=(jax...  1.14 us

profile of v3, /device:TPU:0, one launch (start us, length us, event | category | flops | bytes accessed | tf_op | source)
XLA Modules:
  0.0 43.1 jit_solution(16565214318095589302)
XLA Ops:
  0.6 41.3 %fused_block.1 = (f32[1,72,128]{2,1,0:T(8,128)S(1)}, f32[1,72,2560]{2,1,0:T(8,128)S(1)}, bf16[192,2560]{1,0:T(8,128)(2,1)S(1)}, f32[6,16,20]{2,1,0:T(8,128)S(1)}) custom-call(f32[6,20,384]{2,1,0:T(8,128)} %refs_0_.1, f32[384]{0:T(512)} %refs_1_.1, f32[384]{0:T(512)} %refs_2_.1, f32[9,96,192]{2,1,0:T(8,128)} %bitcast.9, f32[384]{0:T(512)} %refs_4_.1, ...), custom_call_target="tpu_custom_call" | custom-call | tf_op jit(solution)/shard_map/fused_block/pallas_call | solution.py:1082
  41.9 1.1 %finish_tokens.1 = (f32[3,20,1,2560]{3,2,1,0:T(1,128)}, f32[6,16,20]{2,1,0:T(8,128)}) custom-call(f32[1,72,128]{2,1,0:T(8,128)S(1)} %get-tuple-element.8.patch, f32[1,72,2560]{2,1,0:T(8,128)S(1)} %get-tuple-element.9.base, bf16[192,2560]{1,0:T(8,128)(2,1)S(1)} %get-tuple-element.10.wc, f32[6,16,20]{2,1,0:T(8,128)S(1)} %get-tuple-element.11.latent_in), custom_call_target="tpu_custom_call" | custom-call | tf_op jit(solution)/shard_map/finish_tokens/pallas_call | solution.py:1099

commit v4 on v3

--- a/solution.py
+++ b/solution.py
@@ -376,38 +376,44 @@
             for tap in range(9):
                 v.mat[k, q, tap * LANES + CB : (tap + 1) * LANES, :] = gap
 
-    def z_copy(k, n, peer, slot, cc):
+    WH = up(WM // 2, 8)
+    pieces_of = (pl.ds(0, WH), pl.ds(WH, WM - WH))
+    order = (far, far2, pair)
+
+    def z_copy(k, n, peer, slot, cc, h):
         return remote(
-            v.wpack.at[k, lax.rem(peer, 2), cc], v.wq.at[k, slot, 2 * g + cc],
-            v.zs.at[0], v.zr.at[k, n], space=peer, chan=cc,
-        )
-
-    def y_copy(k, n, z, which):
-        ref = v.wq.at[k, z, which]
-        return remote(ref, ref, v.ys.at[0], v.yr.at[k, n], groups=gy)
-
-    def b_copy(k, n, z, which):
-        ref = v.wq.at[k, z, which]
+            v.wpack.at[k, lax.rem(peer, 2), cc, pieces_of[h]],
+            v.wq.at[k, slot, 2 * g + cc, pieces_of[h]],
+            v.zs.at[0], v.zr.at[k, n, h], space=peer, chan=cc,
+        )
+
+    def y_copy(k, n, z, which, h):
+        ref = v.wq.at[k, z, which, pieces_of[h]]
+        return remote(ref, ref, v.ys.at[0], v.yr.at[k, n, h], groups=gy)
+
+    def b_copy(k, n, z, which, h):
+        ref = v.wq.at[k, z, which, pieces_of[h]]
         return remote(ref, ref, v.bs.at[0], v.br.at[k, n], chan=oc)
 
-    order = (far, far2, pair)
-
     def z_send(k, n):
-        for cc in range(C):
-            go_if(home, z_copy(k, n, order[n], s, cc))
+        for h in range(2):
+            for cc in range(C):
+                go_if(home, z_copy(k, n, order[n], s, cc, h))
 
     def relay(k, n):
         z = order[n]
-        remote(
-            v.wpack.at[k, 0, 0], v.wq.at[k, z, 2 * g + c], v.zs.at[0], v.zr.at[k, n],
-            space=z, chan=t,
-        ).wait_recv()
-        y_copy(k, n, z, 2 * g + c).start()
-        b_copy(k, n, z, 2 * g + c).start()
+        for h in range(2):
+            remote(
+                v.wpack.at[k, 0, 0, pieces_of[h]], v.wq.at[k, z, 2 * g + c, pieces_of[h]],
+                v.zs.at[0], v.zr.at[k, n, h], space=z, chan=t,
+            ).wait_recv()
+            y_copy(k, n, z, 2 * g + c, h).start()
+            b_copy(k, n, z, 2 * g + c, h).start()
 
     def relay2(k, n, z):
-        y_copy(k, n, z, 2 * gy + c).wait_recv()
-        b_copy(k, n, z, 2 * gy + c).start()
+        for h in range(2):
+            y_copy(k, n, z, 2 * gy + c, h).wait_recv()
+            b_copy(k, n, z, 2 * gy + c, h).start()
 
     def nth_weights(i):
         flip = lax.rem(lax.div(i + 1, 2), 2)
@@ -646,7 +652,7 @@
         def _():
             relay2(0, i + 1, nth_weights(i + 2))
 
-        @pl.when(i == 2)
+        @pl.when(i == 1)
         def _():
             relay(1, 0)
 
@@ -709,6 +715,7 @@
     own_mat(1)
     relay(1, 2)
     relay(1, 1)
+    relay2(1, 0, far)
     center, inverse = rim_finish(0, *rims1)
     v.rl_in[own, 0 : 2 * R, :] = v.colm_in[0, 0 : 2 * R, :]
     v.rl_in[own, 2 * R : 2 * R + 1, :] = v.corm_in[0, 0:1, :]
@@ -738,12 +745,23 @@
 
         @pl.when(j == 1)
         def _():
-            relay2(1, 2, pair)
+            relay2(1, 1, far2)
+
+        @pl.when(j == 2)
+        def _():
+            finish_weights(1, 2 - lax.rem(t + hh, 2), near)
+
+        @pl.when(j == 3)
+        def _():
+            finish_weights(1, 1 + lax.rem(t + hh, 2), cross)
+
+        @pl.when((j == 1) & (t == hh))
+        def _():
+            finish_weights(1, 0, far)
+
+        @pl.when(j == 1)
+        def _():
             rl_copy(2, side, tm=tx).wait_recv()
-
-        @pl.when(j == 2)
-        def _():
-            relay2(1, 1, far2)
 
         @pl.when(j == 2)
         def _():
@@ -768,26 +786,15 @@
 
         second_taps(q)
 
+        @pl.when((j == 0) & (t != hh))
+        def _():
+            finish_weights(1, 0, far)
+
+        v.acc[...] += conv_block(1, q)
+
         @pl.when(j == 0)
         def _():
-            relay2(1, 0, far)
-
-        @pl.when(j == jnp.where(t == hh, 1, 0))
-        def _():
-            finish_weights(1, 0, far)
-
-        @pl.when(j == 2)
-        def _():
-            finish_weights(1, 2 - lax.rem(t + hh, 2), near)
-
-        @pl.when(j == 3)
-        def _():
-            finish_weights(1, 1 + lax.rem(t + hh, 2), cross)
-
-        v.acc[...] += conv_block(1, q)
-
-        @pl.when(j == 0)
-        def _():
+            relay2(1, 2, pair)
             side_copy.wait_recv()
             cross_z.start()
             near_copy.wait_recv()
@@ -1069,8 +1076,8 @@
         "rs_sem": dma(2), "rr_sem": dma(2),
         "os_sem": dma(1), "or_sem": dma(1),
         "is_sem": dma(1), "ir_sem": dma(1),
-        "zs": dma(1), "zr": dma(2, 3),
-        "ys": dma(1), "yr": dma(2, 3),
+        "zs": dma(1), "zr": dma(2, 3, 2),
+        "ys": dma(1), "yr": dma(2, 3, 2),
         "bs": dma(1), "br": dma(2, 3),
         "es": dma(1), "er": dma(2),
         "ks": dma(1), "kr": dma(2),

time: 43.2 us -> 42.3 us (0.979)
  Pallas kernels: 42.4 us -> 41.5 us
    pallas_call x1, Pallas kernels: 41.3 us -> 40.4 us  [fused(): pl.pallas_call(functools.partial(fused_kernel, dims, tuple(scratch)), out...]
where the time goes in v4:
time: 42.3 us; the launch traced here: 42.2 us
  Pallas kernels  41.5 us (98%)
  between operations  0.64 us (2%)
    pallas_call x1, Pallas kernels, fused(): pl.pallas_call(functools.partial(fused_kernel, dims, tuple(scratch)), out...  40.4 us
    pallas_call x1, Pallas kernels, fused(): pl.pallas_call(functools.partial(finish_kernel, dims, NB), out_shape=(jax...  1.12 us

profile of v4, /device:TPU:0, one launch (start us, length us, event | category | flops | bytes accessed | tf_op | source)
XLA Modules:
  0.0 42.2 jit_solution(7987976305482747174)
XLA Ops:
  0.6 40.4 %fused_block.1 = (f32[1,72,128]{2,1,0:T(8,128)S(1)}, f32[1,72,2560]{2,1,0:T(8,128)S(1)}, bf16[192,2560]{1,0:T(8,128)(2,1)S(1)}, f32[6,16,20]{2,1,0:T(8,128)S(1)}) custom-call(f32[6,20,384]{2,1,0:T(8,128)} %refs_0_.1, f32[384]{0:T(512)} %refs_1_.1, f32[384]{0:T(512)} %refs_2_.1, f32[9,96,192]{2,1,0:T(8,128)} %bitcast.9, f32[384]{0:T(512)} %refs_4_.1, ...), custom_call_target="tpu_custom_call" | custom-call | tf_op jit(solution)/shard_map/fused_block/pallas_call | solution.py:1089
  41.0 1.1 %finish_tokens.1 = (f32[3,20,1,2560]{3,2,1,0:T(1,128)}, f32[6,16,20]{2,1,0:T(8,128)}) custom-call(f32[1,72,128]{2,1,0:T(8,128)S(1)} %get-tuple-element.8.patch, f32[1,72,2560]{2,1,0:T(8,128)S(1)} %get-tuple-element.9.base, bf16[192,2560]{1,0:T(8,128)(2,1)S(1)} %get-tuple-element.10.wc, f32[6,16,20]{2,1,0:T(8,128)S(1)} %get-tuple-element.11.latent_in), custom_call_target="tpu_custom_call" | custom-call | tf_op jit(solution)/shard_map/finish_tokens/pallas_call | solution.py:1106

commit v5 on v4

--- a/solution.py
+++ b/solution.py
@@ -445,11 +445,12 @@
             v.a_pack.at[blocks], v.a_in.at[p, blocks], v.fs.at[0], v.fr.at[m], space=pair
         )
 
-    def st_copy(dt, peer, mt, ms):
-        return remote(
-            v.st, v.st_in.at[mt, ms], v.ss_sem.at[0], v.sr_sem.at[0],
-            space=peer, tm=tx if dt else t,
-        )
+    def st_copy(peer):
+        return remote(v.st, v.st_in.at[t, s], v.ss_sem.at[0], v.sr_sem.at[0], space=peer)
+
+    st_forward = remote(
+        v.st_in.at[t], v.st_in.at[t], v.ss_sem.at[0], v.sr_sem.at[1], tm=tx
+    )
 
     def col_copy(n, slot, **where):
         return remote(v.colf, v.colf_in.at[slot], v.cs_sem.at[0], v.cr_sem.at[slot], **where)
@@ -463,10 +464,9 @@
     def cor_copy(n, **where):
         return remote(v.corf, v.corf_in, v.os_sem.at[0], v.or_sem.at[0], **where)
 
-    st_peers = [(0, far), (0, far2), (1, far), (1, far2), (0, pair), (1, pair), (1, s)]
     go_if(hub, row_copy)
-    for dt, peer in st_peers:
-        go(st_copy(dt, peer, t, s))
+    for peer in order:
+        go(st_copy(peer))
     for n, (peer, column) in enumerate(((far, t), (far2, t), (far, tx), (far2, tx))):
         go_if(inner & stray, cor_copy(n, space=peer, tm=column))
     go_if(stray, col_copy(0, p, tm=tx))
@@ -523,6 +523,8 @@
                 feat_part(m).wait_recv()
                 feat_pass(m).start()
 
+    await_bytes(rows_of(8 * (S - 1)), v.sr_sem.at[0])
+    go(st_forward)
     pass_features(inner)
     relay(0, 0)
     pass_features(jnp.logical_not(inner))
@@ -556,7 +558,7 @@
             feat_pass(m).wait_recv()
 
     unpack_features(1 - p)
-    await_bytes(rows_of(8 * len(st_peers)), v.sr_sem.at[0])
+    await_bytes(rows_of(8 * S), v.sr_sem.at[1])
     col_copy(1, 1 - p, space=pair).wait_recv()
     pl.when(home)(col_copy(0, p, tm=tx).wait_recv)
     cor_copy(0, space=far).wait_recv()
@@ -925,7 +927,7 @@
     RR = up(W + 2, 8)
     drains = (
         (home, rows_of(S * AM), v.as_sem), (home, rows_of(S * AM), v.fs),
-        (home, rows_of(S * AM), v.gs), (None, rows_of(8 * len(st_peers)), v.ss_sem),
+        (home, rows_of(S * AM), v.gs), (None, rows_of(8 * (2 * S - 1)), v.ss_sem),
         (stray, rows_of(3 * S * 8), v.cs_sem), (hub, rows_of(S * RR), v.rs_sem),
         (inner & stray, rows_of(4 * 8), v.os_sem), (None, rows_of(ZH), v.is_sem),
         (home, v.wq.at[0, pl.ds(0, 3)], v.zs), (None, v.wq.at[0, pl.ds(0, 3), pl.ds(0, 2)], v.ys),
@@ -1071,7 +1073,7 @@
         "patch": buf(PR * PP, LANES),
         "load_sem": dma(15),
         "as_sem": dma(1), "ar_sem": dma(1), "fs": dma(1), "fr": dma(2), "gs": dma(1),
-        "ss_sem": dma(1), "sr_sem": dma(1),
+        "ss_sem": dma(1), "sr_sem": dma(2),
         "cs_sem": dma(1), "cr_sem": dma(2),
         "rs_sem": dma(2), "rr_sem": dma(2),
         "os_sem": dma(1), "or_sem": dma(1),

time: 42.3 us -> 42 us (level)
  no operation moved by 1% of the time
where the time goes in v5:
time: 42 us; the launch traced here: 41.9 us
  Pallas kernels  41.2 us (98%)
  between operations  0.64 us (2%)
    pallas_call x1, Pallas kernels, fused(): pl.pallas_call(functools.partial(fused_kernel, dims, tuple(scratch)), out...  40.1 us
    pallas_call x1, Pallas kernels, fused(): pl.pallas_call(functools.partial(finish_kernel, dims, NB), out_shape=(jax...  1.14 us

profile of v5, /device:TPU:0, one launch (start us, length us, event | category | flops | bytes accessed | tf_op | source)
XLA Modules:
  0.0 41.9 jit_solution(12891448364080544625)
XLA Ops:
  0.6 40.1 %fused_block.1 = (f32[1,72,128]{2,1,0:T(8,128)S(1)}, f32[1,72,2560]{2,1,0:T(8,128)S(1)}, bf16[192,2560]{1,0:T(8,128)(2,1)S(1)}, f32[6,16,20]{2,1,0:T(8,128)S(1)}) custom-call(f32[6,20,384]{2,1,0:T(8,128)} %refs_0_.1, f32[384]{0:T(512)} %refs_1_.1, f32[384]{0:T(512)} %refs_2_.1, f32[9,96,192]{2,1,0:T(8,128)} %bitcast.9, f32[384]{0:T(512)} %refs_4_.1, ...), custom_call_target="tpu_custom_call" | custom-call | tf_op jit(solution)/shard_map/fused_block/pallas_call | solution.py:1091
  40.7 1.1 %finish_tokens.1 = (f32[3,20,1,2560]{3,2,1,0:T(1,128)}, f32[6,16,20]{2,1,0:T(8,128)}) custom-call(f32[1,72,128]{2,1,0:T(8,128)S(1)} %get-tuple-element.8.patch, f32[1,72,2560]{2,1,0:T(8,128)S(1)} %get-tuple-element.9.base, bf16[192,2560]{1,0:T(8,128)(2,1)S(1)} %get-tuple-element.10.wc, f32[6,16,20]{2,1,0:T(8,128)S(1)} %get-tuple-element.11.latent_in), custom_call_target="tpu_custom_call" | custom-call | tf_op jit(solution)/shard_map/finish_tokens/pallas_call | solution.py:1108
